TPU v7x, 256 devices: a whole 4x4x8 slice. The times are simulated.
256 devices in a mesh: tm: 32 (over x, z), phase: 8 (over y, core).
Axes of the slice: x: 4, y: 4, z: 8, core: 2. Of those that a mesh axis runs over, the one named last changes fastest.
Arguments:
- frames: bfloat16 [2, 4096, 1024], P(None, 'tm'), may hold values from -6 to 6
- frame_counts: int32 [2, 128], replicated, may hold values from 1 to 32, as said below
- w_query: bfloat16 [8, 1024, 1024], P('phase')
- w_key: bfloat16 [8, 1024, 1024], P('phase')
- w_value: bfloat16 [8, 1024, 1024], P('phase'), may hold values from -0.1875 to 0.1875
- w_out: bfloat16 [8, 1024, 1024], P('phase'), may hold values from -0.1875 to 0.1875
- conv_kernel: bfloat16 [8, 31, 1024], P('phase'), may hold values from -1 to 1
- w_point: bfloat16 [8, 1024, 1024], P('phase'), may hold values from -0.1875 to 0.1875
Outputs:
- layer_outputs: bfloat16 [8, 2, 4096, 1024], P('phase', None, 'tm')
Inputs may be any that keep to these rules, and one draw needn't show every extreme that they name: `frame_counts`: A segment's valid frames are its first ones; the largest count 32 occurs in every draw.
All inputs are finite; a program needn't handle non-finite values.
Results may differ from a plain program's by a relative error of at most 0.034.
Values may be sent and summed in bfloat16 or wider, within the bound.
A program may use at most 64 MiB of HBM per device.

v0:
```python
import math

import jax
import jax.numpy as jnp
from jax import lax
from jax.sharding import PartitionSpec as P

HEADS = 16
SEG = 32
LC = 64
NMEM = 4
KW = 31
SEG_MB = 4


EPSILON = 1e-05


def from_behind(block, axis, distance):
    devices = range(lax.axis_size(axis))
    route = [((i - distance) % len(devices), i) for i in devices]
    return lax.ppermute(block, axis, route)


def passed_along(block, axis, distance):
    devices = range(lax.axis_size(axis))
    route = [(i - distance, i) for i in devices if i - distance in devices]
    return lax.ppermute(block, axis, route)


def layer_norm(values):
    center = values - jnp.mean(values, axis=-1, keepdims=True)
    spread = jnp.mean(center * center, axis=-1, keepdims=True)
    return center * lax.rsqrt(spread + EPSILON)


def attend_blocks(queries, blocks):
    query_len, model_width = queries.shape
    head_dim = model_width // HEADS
    split_q = queries.reshape(query_len, HEADS, head_dim)
    score_list = []
    for key_rows, value_rows, allowed in blocks:
        split_k = key_rows.reshape(key_rows.shape[0], HEADS, head_dim)
        scores = jnp.einsum(
            "qhd,khd->hqk", split_q, split_k, preferred_element_type=jnp.float32
        ) / math.sqrt(head_dim)
        score_list.append(jnp.where(allowed[None, :, :], scores, -1e30))
    top_score = score_list[0].max(axis=-1, keepdims=True)
    for scores in score_list[1:]:
        top_score = jnp.maximum(top_score, scores.max(axis=-1, keepdims=True))
    exp_list = [jnp.exp(scores - top_score) for scores in score_list]
    total = exp_list[0].sum(axis=-1, keepdims=True)
    for exponent in exp_list[1:]:
        total = total + exponent.sum(axis=-1, keepdims=True)
    context = jnp.zeros((query_len, HEADS, head_dim), jnp.float32)
    for exponent, block in zip(exp_list, blocks):
        weights = (exponent / total).astype(jnp.bfloat16)
        split_v = block[1].reshape(block[1].shape[0], HEADS, head_dim)
        context = context + jnp.einsum(
            "hqk,khd->qhd", weights, split_v, preferred_element_type=jnp.float32
        )
    return context.reshape(query_len, model_width)


def settle(received, stashed, leading):
    return jax.tree.map(
        lambda current, earlier: jnp.where(leading, earlier, current), received, stashed
    )


def project(rows_in, weight):
    return jnp.dot(rows_in, weight, preferred_element_type=jnp.float32).astype(jnp.bfloat16)


def per_device(frames, frame_counts, w_query, w_key, w_value, w_out, conv_kernel, w_point):
    micro_count, row_count, model_width = frames.shape
    phase_count = lax.axis_size("phase")
    shard_count = lax.axis_size("tm")
    phase_id = lax.axis_index("phase")
    shard_id = lax.axis_index("tm")
    query_weight = w_query[0]
    key_weight = w_key[0]
    value_weight = w_value[0]
    out_weight = w_out[0]
    kernel = conv_kernel[0].astype(jnp.float32)
    point_weight = w_point[0]
    padded_counts = jnp.concatenate([jnp.zeros((SEG_MB,), jnp.int32), frame_counts.reshape(-1)])
    leading = shard_id == 0
    own_index = jnp.arange(row_count, dtype=jnp.int32)
    left_index = jnp.arange(LC, dtype=jnp.int32)
    slot_index = jnp.arange(2 * SEG_MB, dtype=jnp.int32)
    frame_segment = own_index // SEG
    block_segment = jnp.arange(SEG_MB, dtype=jnp.int32)

    def masks(segment_ids, own_valid, left_valid, slot_live):
        first_frame = segment_ids[:, None] * SEG
        own_ok = (
            (own_index[None, :] >= first_frame - LC)
            & (own_index[None, :] < first_frame + SEG)
            & own_valid[None, :]
        )
        left_ok = (left_index[None, :] - LC >= first_frame - LC) & left_valid[None, :]
        slot_ok = (
            (slot_index[None, :] >= segment_ids[:, None] + SEG_MB - NMEM)
            & (slot_index[None, :] < segment_ids[:, None] + SEG_MB)
            & slot_live[None, :]
        )
        return (own_ok, left_ok, slot_ok)

    def empty_rows(count):
        return jnp.zeros((count, model_width), jnp.bfloat16)

    context_init = (empty_rows(LC), empty_rows(LC))
    memory_init = (empty_rows(SEG_MB), empty_rows(SEG_MB))

    def one_step(step_index, state_tuple):
        inbox, context_stash, memory_stash, rim_stash, outputs = state_tuple
        position = step_index - phase_id
        active = (position >= 0) & (position < micro_count)
        clipped = jnp.clip(position, 0, micro_count - 1)
        own_input = lax.dynamic_index_in_dim(frames, clipped, 0, keepdims=False)
        layer_input = jnp.where(phase_id == 0, own_input, inbox)
        first_segment = clipped * (shard_count * SEG_MB) + shard_id * SEG_MB
        near_counts = lax.dynamic_slice_in_dim(padded_counts, first_segment, 2 * SEG_MB)
        frame_mask = jnp.arange(SEG, dtype=jnp.int32)[None, :] < near_counts[:, None]
        own_valid = frame_mask[SEG_MB:].reshape(-1)
        left_valid = frame_mask[:SEG_MB].reshape(-1)[SEG_MB * SEG - LC :]
        slot_live = near_counts > 0
        row_mask = own_valid.astype(jnp.float32).reshape(row_count, 1)
        inputs = layer_input.astype(jnp.float32)
        normed = layer_norm(inputs).astype(jnp.bfloat16)
        queries = project(normed, query_weight)
        key_own = project(normed, key_weight)
        value_own = project(normed, value_weight)
        received = from_behind((key_own[row_count - LC :], value_own[row_count - LC :]), "tm", 1)
        key_left, value_left = settle(received, context_stash, leading)
        seg_rows = normed.reshape(SEG_MB, SEG, model_width).astype(jnp.float32)
        own_mask = frame_mask[SEG_MB:].astype(jnp.float32)
        own_counts = near_counts[SEG_MB:].astype(jnp.float32)
        summary = (jnp.sum(seg_rows * own_mask[:, :, None], axis=1) / own_counts[:, None]).astype(
            jnp.bfloat16
        )
        summary_q = project(summary, query_weight)
        sum_own_ok, sum_left_ok, unused_ok = masks(block_segment, own_valid, left_valid, slot_live)
        memory = attend_blocks(
            summary_q, [(key_left, value_left, sum_left_ok), (key_own, value_own, sum_own_ok)]
        ).astype(jnp.bfloat16)
        mem_key_own = project(memory, key_weight)
        mem_value_own = project(memory, value_weight)
        received_mem = from_behind((mem_key_own, mem_value_own), "tm", 1)
        mem_key_prev, mem_value_prev = settle(received_mem, memory_stash, leading)
        own_ok, left_ok, slot_ok = masks(frame_segment, own_valid, left_valid, slot_live)
        context = attend_blocks(
            queries,
            [
                (mem_key_prev, mem_value_prev, slot_ok[:, :SEG_MB]),
                (mem_key_own, mem_value_own, slot_ok[:, SEG_MB:]),
                (key_left, value_left, left_ok),
                (key_own, value_own, own_ok),
            ],
        )
        context = context.astype(jnp.bfloat16)
        residual = (
            inputs + jnp.dot(context, out_weight, preferred_element_type=jnp.float32)
        ).astype(jnp.bfloat16)
        conv_in = (layer_norm(residual.astype(jnp.float32)) * row_mask).astype(jnp.bfloat16)
        received_rim = from_behind(conv_in[row_count - (KW - 1) :], "tm", 1)
        rim_rows = jnp.where(leading, rim_stash, received_rim)
        rim_rows = jnp.where(leading & (clipped == 0), jnp.zeros_like(rim_rows), rim_rows)
        extended = jnp.concatenate([rim_rows, conv_in])
        depth = jnp.zeros((row_count, model_width), jnp.float32)
        for offset in range(KW):
            depth = depth + kernel[offset] * extended[offset : offset + row_count].astype(
                jnp.float32
            )
        gated = jax.nn.silu(layer_norm(depth)).astype(jnp.bfloat16)
        mixed = residual.astype(jnp.float32) + jnp.dot(
            gated, point_weight, preferred_element_type=jnp.float32
        )
        result = (mixed * row_mask).astype(jnp.bfloat16)
        existing = lax.dynamic_index_in_dim(outputs, clipped, 0, keepdims=False)
        outputs = lax.dynamic_update_index_in_dim(
            outputs, jnp.where(active, result, existing), clipped, 0
        )
        next_inbox = passed_along(result, "phase", 1)
        return (next_inbox, received, received_mem, received_rim, outputs)

    start_state = (
        empty_rows(row_count),
        context_init,
        memory_init,
        empty_rows(KW - 1),
        jnp.zeros((micro_count, row_count, model_width), jnp.bfloat16),
    )
    final_state = lax.fori_loop(0, micro_count + phase_count - 1, one_step, start_state)
    return final_state[4][None]


def solution(mesh):
    in_specs = (
        P(None, "tm", None),
        P(),
        P("phase", None, None),
        P("phase", None, None),
        P("phase", None, None),
        P("phase", None, None),
        P("phase", None, None),
        P("phase", None, None),
    )
    out_specs = P("phase", None, "tm", None)
    return jax.shard_map(
        per_device, mesh=mesh, in_specs=in_specs, out_specs=out_specs, check_vma=False
    )
```

profile of v0, /device:TPU:1, one launch (start us, length us, event | category | flops | bytes accessed | tf_op | source)
XLA Modules:
  0.0 700.0 jit_solution(6504682771496753923)
XLA Ops:
  6.9 693.1 %while.32 = (s32[]{:T(128)}, bf16[128,1024]{1,0:T(8,128)(2,1)S(1)}, bf16[64,1024]{1,0:T(8,128)(2,1)}, bf16[64,1024]{1,0:T(8,128)(2,1)}, bf16[4,1024]{1,0:T(4,128...) while((s32[]{:T(128)}, bf16[128,1024]{1,0:T(8,128)(2,1)S(1)}, ...), condition=%wide.region_20.21_spmd.clone.clone, body=%wide.region_0.20_spmd.clone.clone.sunk | while | flops 1509182336 | bytes 101471064 | solution.py:195
  67.4 6.4 collective-permute-done.4
  77.5 6.7 collective-permute-start.5
  144.6 7.0 %collective-permute-done.4 = bf16[30,1024]{1,0:T(8,128)(2,1)S(1)} collective-permute-done((bf16[30,1024]{1,0:T(8,128)(2,1)S(1)}, bf16[30,1024]{1,0:T(8,128)(2,1)S(1)}, u32[]{:S(2)}, u32[]{:S(2)}) %collective-permute-start.4) | collective-permute-done | bytes 61472 | tf_op jit(solution)/shard_map/while/body/eval_jaxpr/ppermute | solution.py:22
  155.3 5.3 collective-permute-start.5
  210.7 4.9 collective-permute-done.2
  221.1 6.4 collective-permute-done.4
  231.1 5.9 collective-permute-start.5
  287.2 4.9 collective-permute-done.2
  297.5 6.4 collective-permute-done.4
  307.6 5.9 collective-permute-start.5
  363.7 4.9 collective-permute-done.2
  374.0 6.4 collective-permute-done.4
  384.1 5.9 collective-permute-start.5
  450.5 6.4 collective-permute-done.4
  460.6 5.9 collective-permute-start.5
  516.6 4.9 collective-permute-done.2
  527.0 6.4 collective-permute-done.4
  537.1 5.9 collective-permute-start.5
  603.5 6.4 collective-permute-done.4
  613.5 5.9 collective-permute-start.5
  669.6 4.9 collective-permute-done.2
  680.0 6.4 collective-permute-done.4
  690.0 5.9 collective-permute-start.5
  (1930 shorter events, 555.1 us)
Async XLA Ops:
  13.3 29.4 %collective-permute-start = (bf16[64,1024]{1,0:T(8,128)(2,1)}, bf16[64,1024]{1,0:T(8,128)(2,1)S(1)}, u32[]{:S(2)}, u32[]{:S(2)}) collective-permute-start(bf16[64,1024]{1,0:T(8,128)(2,1)} %slice.1567), channel_id=1, source_target_pairs={{248,0},{0,8},{8,16},{16,24},{24,32},{32,40},{40,48},{48,56},{56,6... | collective-permute-start | bytes 393224 | tf_op jit(solution)/shard_map/while/body/eval_jaxpr/ppermute | solution.py:22
  16.9 32.0 %collective-permute-start.1 = (bf16[64,1024]{1,0:T(8,128)(2,1)}, bf16[64,1024]{1,0:T(8,128)(2,1)}, u32[]{:S(2)}, u32[]{:S(2)}) collective-permute-start(bf16[64,1024]{1,0:T(8,128)(2,1)} %slice.1569), channel_id=1, source_target_pairs={{248,0},{0,8},{8,16},{16,24},{24,32},{32,40},{40,48},{48,56},{56,6... | collective-permute-start | bytes 393224 | tf_op jit(solution)/shard_map/while/body/eval_jaxpr/ppermute | solution.py:22
  77.5 10.7 %collective-permute-start.5 = (bf16[128,1024]{1,0:T(8,128)(2,1)S(1)}, bf16[128,1024]{1,0:T(8,128)(2,1)S(1)}, u32[]{:S(2)}, u32[]{:S(2)}) collective-permute-start(bf16[128,1024]{1,0:T(8,128)(2,1)S(1)} %get-tuple-element.1277), channel_id=1, source_target_pairs={{0,1},{1,2},{2,3},{3,4},{4,5},{5,6},{6,7},{8,9},{9,10},{10,11},{11... | collective-permute-start | bytes 786440 | tf_op jit(solution)/shard_map/while/body/eval_jaxpr/ppermute | solution.py:28
  94.6 25.3 %collective-permute-start = (bf16[64,1024]{1,0:T(8,128)(2,1)}, bf16[64,1024]{1,0:T(8,128)(2,1)S(1)}, u32[]{:S(2)}, u32[]{:S(2)}) collective-permute-start(bf16[64,1024]{1,0:T(8,128)(2,1)} %slice.1567), channel_id=1, source_target_pairs={{248,0},{0,8},{8,16},{16,24},{24,32},{32,40},{40,48},{48,56},{56,6... | collective-permute-start | bytes 393224 | tf_op jit(solution)/shard_map/while/body/eval_jaxpr/ppermute | solution.py:22
  95.7 30.3 %collective-permute-start.1 = (bf16[64,1024]{1,0:T(8,128)(2,1)}, bf16[64,1024]{1,0:T(8,128)(2,1)}, u32[]{:S(2)}, u32[]{:S(2)}) collective-permute-start(bf16[64,1024]{1,0:T(8,128)(2,1)} %slice.1569), channel_id=1, source_target_pairs={{248,0},{0,8},{8,16},{16,24},{24,32},{32,40},{40,48},{48,56},{56,6... | collective-permute-start | bytes 393224 | tf_op jit(solution)/shard_map/while/body/eval_jaxpr/ppermute | solution.py:22
  171.1 25.3 %collective-permute-start = (bf16[64,1024]{1,0:T(8,128)(2,1)}, bf16[64,1024]{1,0:T(8,128)(2,1)S(1)}, u32[]{:S(2)}, u32[]{:S(2)}) collective-permute-start(bf16[64,1024]{1,0:T(8,128)(2,1)} %slice.1567), channel_id=1, source_target_pairs={{248,0},{0,8},{8,16},{16,24},{24,32},{32,40},{40,48},{48,56},{56,6... | collective-permute-start | bytes 393224 | tf_op jit(solution)/shard_map/while/body/eval_jaxpr/ppermute | solution.py:22
  172.2 30.3 %collective-permute-start.1 = (bf16[64,1024]{1,0:T(8,128)(2,1)}, bf16[64,1024]{1,0:T(8,128)(2,1)}, u32[]{:S(2)}, u32[]{:S(2)}) collective-permute-start(bf16[64,1024]{1,0:T(8,128)(2,1)} %slice.1569), channel_id=1, source_target_pairs={{248,0},{0,8},{8,16},{16,24},{24,32},{32,40},{40,48},{48,56},{56,6... | collective-permute-start | bytes 393224 | tf_op jit(solution)/shard_map/while/body/eval_jaxpr/ppermute | solution.py:22
  231.1 10.0 %collective-permute-start.5 = (bf16[128,1024]{1,0:T(8,128)(2,1)S(1)}, bf16[128,1024]{1,0:T(8,128)(2,1)S(1)}, u32[]{:S(2)}, u32[]{:S(2)}) collective-permute-start(bf16[128,1024]{1,0:T(8,128)(2,1)S(1)} %get-tuple-element.1277), channel_id=1, source_target_pairs={{0,1},{1,2},{2,3},{3,4},{4,5},{5,6},{6,7},{8,9},{9,10},{10,11},{11... | collective-permute-start | bytes 786440 | tf_op jit(solution)/shard_map/while/body/eval_jaxpr/ppermute | solution.py:28
  247.6 25.3 %collective-permute-start = (bf16[64,1024]{1,0:T(8,128)(2,1)}, bf16[64,1024]{1,0:T(8,128)(2,1)S(1)}, u32[]{:S(2)}, u32[]{:S(2)}) collective-permute-start(bf16[64,1024]{1,0:T(8,128)(2,1)} %slice.1567), channel_id=1, source_target_pairs={{248,0},{0,8},{8,16},{16,24},{24,32},{32,40},{40,48},{48,56},{56,6... | collective-permute-start | bytes 393224 | tf_op jit(solution)/shard_map/while/body/eval_jaxpr/ppermute | solution.py:22
  248.7 30.3 %collective-permute-start.1 = (bf16[64,1024]{1,0:T(8,128)(2,1)}, bf16[64,1024]{1,0:T(8,128)(2,1)}, u32[]{:S(2)}, u32[]{:S(2)}) collective-permute-start(bf16[64,1024]{1,0:T(8,128)(2,1)} %slice.1569), channel_id=1, source_target_pairs={{248,0},{0,8},{8,16},{16,24},{24,32},{32,40},{40,48},{48,56},{56,6... | collective-permute-start | bytes 393224 | tf_op jit(solution)/shard_map/while/body/eval_jaxpr/ppermute | solution.py:22
  307.6 10.0 %collective-permute-start.5 = (bf16[128,1024]{1,0:T(8,128)(2,1)S(1)}, bf16[128,1024]{1,0:T(8,128)(2,1)S(1)}, u32[]{:S(2)}, u32[]{:S(2)}) collective-permute-start(bf16[128,1024]{1,0:T(8,128)(2,1)S(1)} %get-tuple-element.1277), channel_id=1, source_target_pairs={{0,1},{1,2},{2,3},{3,4},{4,5},{5,6},{6,7},{8,9},{9,10},{10,11},{11... | collective-permute-start | bytes 786440 | tf_op jit(solution)/shard_map/while/body/eval_jaxpr/ppermute | solution.py:28
  324.1 25.3 %collective-permute-start = (bf16[64,1024]{1,0:T(8,128)(2,1)}, bf16[64,1024]{1,0:T(8,128)(2,1)S(1)}, u32[]{:S(2)}, u32[]{:S(2)}) collective-permute-start(bf16[64,1024]{1,0:T(8,128)(2,1)} %slice.1567), channel_id=1, source_target_pairs={{248,0},{0,8},{8,16},{16,24},{24,32},{32,40},{40,48},{48,56},{56,6... | collective-permute-start | bytes 393224 | tf_op jit(solution)/shard_map/while/body/eval_jaxpr/ppermute | solution.py:22
  325.2 30.3 %collective-permute-start.1 = (bf16[64,1024]{1,0:T(8,128)(2,1)}, bf16[64,1024]{1,0:T(8,128)(2,1)}, u32[]{:S(2)}, u32[]{:S(2)}) collective-permute-start(bf16[64,1024]{1,0:T(8,128)(2,1)} %slice.1569), channel_id=1, source_target_pairs={{248,0},{0,8},{8,16},{16,24},{24,32},{32,40},{40,48},{48,56},{56,6... | collective-permute-start | bytes 393224 | tf_op jit(solution)/shard_map/while/body/eval_jaxpr/ppermute | solution.py:22
  384.1 10.0 %collective-permute-start.5 = (bf16[128,1024]{1,0:T(8,128)(2,1)S(1)}, bf16[128,1024]{1,0:T(8,128)(2,1)S(1)}, u32[]{:S(2)}, u32[]{:S(2)}) collective-permute-start(bf16[128,1024]{1,0:T(8,128)(2,1)S(1)} %get-tuple-element.1277), channel_id=1, source_target_pairs={{0,1},{1,2},{2,3},{3,4},{4,5},{5,6},{6,7},{8,9},{9,10},{10,11},{11... | collective-permute-start | bytes 786440 | tf_op jit(solution)/shard_map/while/body/eval_jaxpr/ppermute | solution.py:28
  400.5 25.3 %collective-permute-start = (bf16[64,1024]{1,0:T(8,128)(2,1)}, bf16[64,1024]{1,0:T(8,128)(2,1)S(1)}, u32[]{:S(2)}, u32[]{:S(2)}) collective-permute-start(bf16[64,1024]{1,0:T(8,128)(2,1)} %slice.1567), channel_id=1, source_target_pairs={{248,0},{0,8},{8,16},{16,24},{24,32},{32,40},{40,48},{48,56},{56,6... | collective-permute-start | bytes 393224 | tf_op jit(solution)/shard_map/while/body/eval_jaxpr/ppermute | solution.py:22
  401.7 30.3 %collective-permute-start.1 = (bf16[64,1024]{1,0:T(8,128)(2,1)}, bf16[64,1024]{1,0:T(8,128)(2,1)}, u32[]{:S(2)}, u32[]{:S(2)}) collective-permute-start(bf16[64,1024]{1,0:T(8,128)(2,1)} %slice.1569), channel_id=1, source_target_pairs={{248,0},{0,8},{8,16},{16,24},{24,32},{32,40},{40,48},{48,56},{56,6... | collective-permute-start | bytes 393224 | tf_op jit(solution)/shard_map/while/body/eval_jaxpr/ppermute | solution.py:22
  460.6 10.0 %collective-permute-start.5 = (bf16[128,1024]{1,0:T(8,128)(2,1)S(1)}, bf16[128,1024]{1,0:T(8,128)(2,1)S(1)}, u32[]{:S(2)}, u32[]{:S(2)}) collective-permute-start(bf16[128,1024]{1,0:T(8,128)(2,1)S(1)} %get-tuple-element.1277), channel_id=1, source_target_pairs={{0,1},{1,2},{2,3},{3,4},{4,5},{5,6},{6,7},{8,9},{9,10},{10,11},{11... | collective-permute-start | bytes 786440 | tf_op jit(solution)/shard_map/while/body/eval_jaxpr/ppermute | solution.py:28
  477.0 25.3 %collective-permute-start = (bf16[64,1024]{1,0:T(8,128)(2,1)}, bf16[64,1024]{1,0:T(8,128)(2,1)S(1)}, u32[]{:S(2)}, u32[]{:S(2)}) collective-permute-start(bf16[64,1024]{1,0:T(8,128)(2,1)} %slice.1567), channel_id=1, source_target_pairs={{248,0},{0,8},{8,16},{16,24},{24,32},{32,40},{40,48},{48,56},{56,6... | collective-permute-start | bytes 393224 | tf_op jit(solution)/shard_map/while/body/eval_jaxpr/ppermute | solution.py:22
  478.1 30.3 %collective-permute-start.1 = (bf16[64,1024]{1,0:T(8,128)(2,1)}, bf16[64,1024]{1,0:T(8,128)(2,1)}, u32[]{:S(2)}, u32[]{:S(2)}) collective-permute-start(bf16[64,1024]{1,0:T(8,128)(2,1)} %slice.1569), channel_id=1, source_target_pairs={{248,0},{0,8},{8,16},{16,24},{24,32},{32,40},{40,48},{48,56},{56,6... | collective-permute-start | bytes 393224 | tf_op jit(solution)/shard_map/while/body/eval_jaxpr/ppermute | solution.py:22
  553.5 25.3 %collective-permute-start = (bf16[64,1024]{1,0:T(8,128)(2,1)}, bf16[64,1024]{1,0:T(8,128)(2,1)S(1)}, u32[]{:S(2)}, u32[]{:S(2)}) collective-permute-start(bf16[64,1024]{1,0:T(8,128)(2,1)} %slice.1567), channel_id=1, source_target_pairs={{248,0},{0,8},{8,16},{16,24},{24,32},{32,40},{40,48},{48,56},{56,6... | collective-permute-start | bytes 393224 | tf_op jit(solution)/shard_map/while/body/eval_jaxpr/ppermute | solution.py:22
  554.6 30.3 %collective-permute-start.1 = (bf16[64,1024]{1,0:T(8,128)(2,1)}, bf16[64,1024]{1,0:T(8,128)(2,1)}, u32[]{:S(2)}, u32[]{:S(2)}) collective-permute-start(bf16[64,1024]{1,0:T(8,128)(2,1)} %slice.1569), channel_id=1, source_target_pairs={{248,0},{0,8},{8,16},{16,24},{24,32},{32,40},{40,48},{48,56},{56,6... | collective-permute-start | bytes 393224 | tf_op jit(solution)/shard_map/while/body/eval_jaxpr/ppermute | solution.py:22
  613.5 10.0 %collective-permute-start.5 = (bf16[128,1024]{1,0:T(8,128)(2,1)S(1)}, bf16[128,1024]{1,0:T(8,128)(2,1)S(1)}, u32[]{:S(2)}, u32[]{:S(2)}) collective-permute-start(bf16[128,1024]{1,0:T(8,128)(2,1)S(1)} %get-tuple-element.1277), channel_id=1, source_target_pairs={{0,1},{1,2},{2,3},{3,4},{4,5},{5,6},{6,7},{8,9},{9,10},{10,11},{11... | collective-permute-start | bytes 786440 | tf_op jit(solution)/shard_map/while/body/eval_jaxpr/ppermute | solution.py:28
  630.0 25.3 %collective-permute-start = (bf16[64,1024]{1,0:T(8,128)(2,1)}, bf16[64,1024]{1,0:T(8,128)(2,1)S(1)}, u32[]{:S(2)}, u32[]{:S(2)}) collective-permute-start(bf16[64,1024]{1,0:T(8,128)(2,1)} %slice.1567), channel_id=1, source_target_pairs={{248,0},{0,8},{8,16},{16,24},{24,32},{32,40},{40,48},{48,56},{56,6... | collective-permute-start | bytes 393224 | tf_op jit(solution)/shard_map/while/body/eval_jaxpr/ppermute | solution.py:22
  631.1 30.3 %collective-permute-start.1 = (bf16[64,1024]{1,0:T(8,128)(2,1)}, bf16[64,1024]{1,0:T(8,128)(2,1)}, u32[]{:S(2)}, u32[]{:S(2)}) collective-permute-start(bf16[64,1024]{1,0:T(8,128)(2,1)} %slice.1569), channel_id=1, source_target_pairs={{248,0},{0,8},{8,16},{16,24},{24,32},{32,40},{40,48},{48,56},{56,6... | collective-permute-start | bytes 393224 | tf_op jit(solution)/shard_map/while/body/eval_jaxpr/ppermute | solution.py:22
  (543 other events, 3513.2 us)
where the time goes:
time: 707 us; the launch traced here: 700 us
  other arithmetic  202 us (29%)
  local copies, waits for them, and re-layouts  168 us (24%)
  matrix products  160 us (23%)
  waiting for transfers between devices  96.7 us (14%)
  starting transfers between devices  65 us (9%)
  loops' own time  8.88 us (1%)
    ppermute x45, waiting for transfers between devices, from_behind(): return lax.ppermute(block, axis, route)  96.6 us
    while x1071, local copies, waits for them, and re-layouts  57.4 us
    ppermute x9, starting transfers between devices, passed_along(): return lax.ppermute(block, axis, route)  53.6 us
    dot_general x54, matrix products, project(): jnp.dot(rows_in, weight, preferred_element_type=jnp.float32)  51.3 us
    dot_general x54, matrix products, attend_blocks(): jnp.einsum('hqk,khd->qhd', weights, split_v, preferred_element_type=jnp.f...  50.7 us
    dot_general x54, matrix products, attend_blocks(): jnp.einsum('qhd,khd->hqk', split_q, split_k, preferred_element_type=jnp.f...  47.2 us
    slice x18, local copies, waits for them, and re-layouts, one_step(): kernel[offset] * extended[offset:offset + row_count].astype(jnp.float32)  33.8 us
    reduce_sum x18, other arithmetic, layer_norm(): center = values - jnp.mean(values, axis=-1, keepdims=True)  33.7 us
  transfers between devices with their start and end apart: 54, of which 18 were waited for; matrix products, arithmetic and copies ran while one was open for 49% of the time, Pallas kernels for 0%

commit v1 on v0

v1 whole, which is shorter than its diff:
```python
import functools

import jax
import jax.numpy as jnp
from jax import lax
from jax.experimental import pallas as pl
from jax.experimental.pallas import tpu as pltpu
from jax.sharding import PartitionSpec as P

HEADS = 16
SEG = 32
LC = 64
NMEM = 4
KW = 31
EPS = 1e-05
NEG = -1e30
F32 = jnp.float32
BF16 = jnp.bfloat16
MESH = pl.DeviceIdType.MESH


def layer_norm(v):
    width = v.shape[-1]
    c = v - jnp.sum(v, axis=-1, keepdims=True) * (1.0 / width)
    s = jnp.sum(c * c, axis=-1, keepdims=True) * (1.0 / width)
    return c * lax.rsqrt(s + EPS)


def dot_nt(a, b):
    return lax.dot_general(a, b, (((1,), (1,)), ((), ())), preferred_element_type=F32)


def dot_nn(a, b):
    return jnp.dot(a, b, preferred_element_type=F32)


def relay_kernel(
    shards, phases, micro, rows, width,
    counts, frames, w_query, w_key, w_value, w_out, w_conv, w_point,
    out,
    wq, wk, wv, wo, wc, wp,
    xin, nbuf, kbuf, vbuf, qbuf, cbuf, rbuf, cext, dbuf, gbuf, obuf, taps,
    mem_out, mem_in, memk, memv, rim_out, rim_in,
    w_sem, fr_sem, out_sem,
    x_send, x_recv, xh_send, xh_recv, mem_send, mem_recv, rim_send, rim_recv,
):
    t = lax.axis_index("tm")
    p = lax.axis_index("phase")
    segs = rows // SEG
    span_segs = shards * segs
    t_next = lax.rem(t + 1, shards)
    t_prev = lax.rem(t + shards - 1, shards)
    p_next = lax.rem(p + 1, phases)
    p_prev = lax.rem(p + phases - 1, phases)
    first_phase = p == 0
    has_next = p < phases - 1
    last_shard = t == shards - 1
    wrap = jnp.where(last_shard, 1, 0)

    loads = [
        pltpu.make_async_copy(src.at[0], dst, w_sem.at[i])
        for i, (src, dst) in enumerate(
            [(w_key, wk), (w_value, wv), (w_query, wq), (w_out, wo), (w_conv, wc), (w_point, wp)]
        )
    ]

    def frame_load(m):
        return pltpu.make_async_copy(frames.at[m], xin.at[m, pl.ds(LC, rows)], fr_sem.at[m])

    @pl.when(first_phase)
    def _():
        for m in range(micro):
            frame_load(m).start()

    for load in loads:
        load.start()

    barrier = pltpu.get_barrier_semaphore()
    for dt, dp in (
        (t_next, p), (t_prev, p), (t, p_next), (t, p_prev), (t_next, p_next), (t_prev, p_prev)
    ):
        pl.semaphore_signal(barrier, inc=1, device_id=(dt, dp), device_id_type=MESH)
    pl.semaphore_wait(barrier, 6)

    def sends_right(m):
        return jnp.logical_or(t < shards - 1, m < micro - 1)

    def has_left(m):
        return jnp.logical_or(t > 0, m > 0)

    def first_halo(m):
        slot = jnp.minimum(m + wrap, micro - 1)
        return pltpu.make_async_remote_copy(
            src_ref=frames.at[m, pl.ds(rows - LC, LC)],
            dst_ref=xin.at[slot, pl.ds(0, LC)],
            send_sem=xh_send.at[micro + m], recv_sem=xh_recv.at[slot],
            device_id=(t_next, p), device_id_type=MESH,
        )

    def block_send(m):
        return pltpu.make_async_remote_copy(
            src_ref=obuf.at[m],
            dst_ref=xin.at[m, pl.ds(LC, rows)],
            send_sem=x_send.at[m], recv_sem=x_recv.at[m],
            device_id=(t, p_next), device_id_type=MESH,
        )

    def to_slot(m):
        return jnp.minimum(m + wrap, micro - 1)

    def halo_send(m, slot):
        return pltpu.make_async_remote_copy(
            src_ref=obuf.at[m, pl.ds(rows - LC, LC)],
            dst_ref=xin.at[slot, pl.ds(0, LC)],
            send_sem=xh_send.at[m], recv_sem=xh_recv.at[slot],
            device_id=(t_next, p_next), device_id_type=MESH,
        )

    def mem_copy(m, slot):
        return pltpu.make_async_remote_copy(
            src_ref=mem_out.at[m], dst_ref=mem_in.at[slot],
            send_sem=mem_send.at[m], recv_sem=mem_recv.at[slot],
            device_id=(t_next, p), device_id_type=MESH,
        )

    def rim_copy(m, slot):
        return pltpu.make_async_remote_copy(
            src_ref=rim_out.at[m], dst_ref=rim_in.at[slot],
            send_sem=rim_send.at[m], recv_sem=rim_recv.at[slot],
            device_id=(t_next, p), device_id_type=MESH,
        )

    def out_copy(m):
        return pltpu.make_async_copy(obuf.at[m], out.at[0, m], out_sem.at[m])

    @pl.when(first_phase)
    def _():
        for m in range(micro):
            @pl.when(sends_right(m))
            def _():
                first_halo(m).start()

    @pl.when(t == 0)
    def _():
        xin[0, 0:LC, :] = jnp.zeros((LC, width), BF16)
        mem_in[0] = jnp.zeros(mem_in.shape[1:], F32)
        rim_in[0] = jnp.zeros(rim_in.shape[1:], BF16)

    loads[4].wait()
    for j in range(KW):
        taps[j] = jnp.broadcast_to(wc[j : j + 1, :].astype(F32), (8, width))

    def count_of(m, rel):
        s = m * span_segs + t * segs + rel
        safe = jnp.maximum(s, 0)
        value = counts[safe // span_segs, lax.rem(safe, span_segs)]
        return jnp.where(s >= 0, value, 0)

    def one_block(m, carry):
        near = [count_of(m, rel) for rel in range(-segs, segs)]
        left = LC // SEG

        @pl.when(first_phase)
        def _():
            frame_load(m).wait()

        @pl.when(jnp.logical_not(first_phase))
        def _():
            block_send(m).wait_recv()

        @pl.when(has_left(m))
        def _():
            halo_send(m, m).wait_recv()

        total = LC + rows

        def norm_rows(i, c):
            r = pl.multiple_of(i * 16, 16)
            nbuf[pl.ds(r, 16), :] = layer_norm(xin[m, pl.ds(r, 16), :].astype(F32)).astype(BF16)
            return c

        lax.fori_loop(0, total // 16, norm_rows, 0, unroll=4)

        srow = lax.broadcasted_iota(jnp.int32, (16, rows), 0)
        scol = lax.broadcasted_iota(jnp.int32, (16, rows), 1)
        cnt_lane = jnp.zeros((16, rows), jnp.int32)
        cnt_col = jnp.ones((16, 1), jnp.int32)
        crow = lax.broadcasted_iota(jnp.int32, (16, 1), 0)
        for i in range(segs):
            cnt_lane = jnp.where(scol // SEG == i, near[segs + i], cnt_lane)
            cnt_col = jnp.where(crow == i, near[segs + i], cnt_col)
        pick = jnp.logical_and(srow == scol // SEG, lax.rem(scol, SEG) < cnt_lane)
        pick = jnp.where(pick, 1.0, 0.0).astype(BF16)
        summary = dot_nn(pick, nbuf[LC:total, :]) / cnt_col.astype(F32)
        nbuf[total : total + 16, :] = summary.astype(BF16)

        @pl.when(m == 0)
        def _():
            for i in (0, 1, 2):
                loads[i].wait()

        def project(n, c):
            col = pl.ds(pl.multiple_of(n * 256, 256), 256)
            kbuf[:, col] = dot_nn(nbuf[0:total, :], wk[:, col]).astype(BF16)
            vbuf[:, col] = dot_nn(nbuf[0:total, :], wv[:, col]).astype(BF16)
            qbuf[:, col] = (dot_nn(nbuf[LC : total + 16, :], wq[:, col]).astype(BF16).astype(F32) * 0.125).astype(BF16)
            return c

        lax.fori_loop(0, width // 256, project, 0)

        nq = segs * HEADS
        hrow = lax.broadcasted_iota(jnp.int32, (HEADS, width), 0)
        hcol = lax.broadcasted_iota(jnp.int32, (HEADS, width), 1) // (width // HEADS)
        head_on = hrow == hcol
        sq = qbuf[rows : rows + 16, :].astype(F32)
        queries = jnp.concatenate(
            [
                jnp.where(head_on, jnp.broadcast_to(sq[i : i + 1, :], (HEADS, width)), 0.0)
                for i in range(segs)
            ],
            axis=0,
        ).astype(BF16)
        mrow = lax.broadcasted_iota(jnp.int32, (nq, total), 0) // HEADS
        mcol = lax.broadcasted_iota(jnp.int32, (nq, total), 1)
        mseg = mcol // SEG
        cnt_key = jnp.zeros((nq, total), jnp.int32)
        for i in range(left + segs):
            cnt_key = jnp.where(mseg == i, near[segs - left + i], cnt_key)
        ok = (mseg >= mrow) & (mseg <= mrow + left) & (lax.rem(mcol, SEG) < cnt_key)
        scores = jnp.where(ok, dot_nt(queries, kbuf[...]), NEG)
        expo = jnp.exp(scores - jnp.max(scores, axis=-1, keepdims=True))
        weights = (expo / jnp.sum(expo, axis=-1, keepdims=True)).astype(BF16)
        mixed = dot_nn(weights, vbuf[...])
        memory = jnp.concatenate(
            [
                jnp.sum(jnp.where(head_on, mixed[i * HEADS : (i + 1) * HEADS, :], 0.0), axis=0, keepdims=True)
                for i in range(segs)
            ]
            + [jnp.zeros((16 - segs, width), F32)],
            axis=0,
        ).astype(BF16)
        gbuf[0:16, :] = memory

        def mem_project(n, c):
            col = pl.ds(pl.multiple_of(n * 256, 256), 256)
            mk = dot_nn(gbuf[0:16, :], wk[:, col]).astype(BF16).astype(F32)
            mv = dot_nn(gbuf[0:16, :], wv[:, col]).astype(BF16).astype(F32)
            mem_out[m, 0:NMEM, col] = mk[0:NMEM]
            mem_out[m, NMEM : 2 * NMEM, col] = mv[0:NMEM]
            return c

        lax.fori_loop(0, width // 256, mem_project, 0)

        @pl.when(sends_right(m))
        def _():
            mem_copy(m, to_slot(m)).start()

        @pl.when(has_left(m))
        def _():
            mem_copy(m, m).wait_recv()

        pad = jnp.zeros((SEG - 2 * NMEM, width), F32)
        memk[...] = jnp.concatenate([mem_in[m, 0:NMEM, :], mem_out[m, 0:NMEM, :], pad], axis=0).astype(BF16)
        memv[...] = jnp.concatenate(
            [mem_in[m, NMEM : 2 * NMEM, :], mem_out[m, NMEM : 2 * NMEM, :], pad], axis=0
        ).astype(BF16)

        quad = 4
        qw = quad * (width // HEADS)
        win = LC + SEG
        lane = lax.broadcasted_iota(jnp.int32, (1, 128), 1)
        lane_seg = lane // SEG
        biases = []
        for i in range(segs):
            cnt = jnp.zeros((1, 128), jnp.int32)
            for j in range(left + 1):
                cnt = jnp.where(lane_seg == j, near[segs - left + i + j], cnt)
            okay = (lane < win) & (lax.rem(lane, SEG) < cnt)
            for j in range(NMEM):
                okay = okay | ((lane == win + i + j) & (near[i + j] > 0))
            biases.append(jnp.where(okay, 0.0, NEG))
        qlane = lax.broadcasted_iota(jnp.int32, (1, qw), 1) // (width // HEADS)
        sel = [jnp.where(qlane == h, 1.0, 0.0).astype(BF16) for h in range(quad)]

        def attend(g, c):
            col = pl.ds(pl.multiple_of(g * qw, qw), qw)
            mk = memk[:, col]
            mv = memv[:, col]
            for i in range(segs):
                q = qbuf[i * SEG : (i + 1) * SEG, col]
                q4 = jnp.concatenate([q * sel[h] for h in range(quad)], axis=0)
                ks = jnp.concatenate([kbuf[i * SEG : i * SEG + win, col], mk], axis=0)
                vs = jnp.concatenate([vbuf[i * SEG : i * SEG + win, col], mv], axis=0)
                s = dot_nt(q4, ks) + biases[i]
                e = jnp.exp(s - jnp.max(s, axis=-1, keepdims=True))
                o = dot_nn(e.astype(BF16), vs) / jnp.sum(e, axis=-1, keepdims=True)
                ctx = jnp.where(qlane == 0, o[0:SEG], 0.0)
                for h in range(1, quad):
                    ctx = jnp.where(qlane == h, o[h * SEG : (h + 1) * SEG], ctx)
                cbuf[i * SEG : (i + 1) * SEG, col] = ctx.astype(BF16)
            return c

        lax.fori_loop(0, width // qw, attend, 0)

        @pl.when(m == 0)
        def _():
            loads[3].wait()

        def project_out(n, c):
            col = pl.ds(pl.multiple_of(n * 256, 256), 256)
            r = xin[m, LC:total, col].astype(F32) + dot_nn(cbuf[...], wo[:, col])
            rbuf[:, col] = r.astype(BF16)
            return c

        lax.fori_loop(0, width // 256, project_out, 0)

        def row_mask(i):
            seg = i // 2
            cnt = count_of(m, seg)
            ids = lax.broadcasted_iota(jnp.int32, (16, 1), 0) + lax.rem(i, 2) * 16
            return jnp.where(ids < cnt, 1.0, 0.0)

        def conv_rows(i, c):
            r = pl.multiple_of(i * 16, 16)
            z = (layer_norm(rbuf[pl.ds(r, 16), :].astype(F32)) * row_mask(i)).astype(BF16)
            cext[pl.ds(r + SEG, 16), :] = z.astype(F32)
            return c

        lax.fori_loop(0, rows // 16, conv_rows, 0, unroll=4)
        rim_out[m] = cext[rows : rows + SEG, :].astype(BF16)

        @pl.when(sends_right(m))
        def _():
            rim_copy(m, to_slot(m)).start()

        sub = lax.broadcasted_iota(jnp.int32, (8, 128), 0)

        def conv_range(k0, k1):
            def body(cb, c):
                col = pl.ds(pl.multiple_of(cb * 128, 128), 128)
                a = {}

                def get(k):
                    if k not in a:
                        a[k] = cext[8 * k : 8 * k + 8, col]
                    return a[k]

                def tap(o):
                    return taps[o - 2, :, col]

                acc = {}
                for s in range(8):
                    offs = [o for o in range(s, KW + 2, 8) if 2 <= o <= KW + 1]
                    prev = None
                    for k in range(k0, k1 + (1 if s else 0)):
                        y = None
                        for o in offs:
                            term = tap(o) * get(k + o // 8)
                            y = term if y is None else y + term
                        if s == 0:
                            acc[k] = y
                            continue
                        y = pltpu.roll(y, 8 - s, axis=0)
                        if prev is not None:
                            acc[k - 1] = acc[k - 1] + jnp.where(sub < 8 - s, prev, y)
                        prev = y
                for k in range(k0, k1):
                    dbuf[8 * k : 8 * k + 8, col] = acc[k]
                return c

            lax.fori_loop(0, width // 128, body, 0)

        conv_range(SEG // 8, rows // 8)

        @pl.when(has_left(m))
        def _():
            rim_copy(m, m).wait_recv()

        cext[0:SEG, :] = rim_in[m].astype(F32)
        conv_range(0, SEG // 8)

        def gate_rows(i, c):
            r = pl.multiple_of(i * 16, 16)
            z = layer_norm(dbuf[pl.ds(r, 16), :])
            gbuf[pl.ds(r, 16), :] = (z / (1.0 + jnp.exp(-z))).astype(BF16)
            return c

        lax.fori_loop(0, rows // 16, gate_rows, 0, unroll=4)

        @pl.when(m == 0)
        def _():
            loads[5].wait()

        vrow = lax.broadcasted_iota(jnp.int32, (rows, 1), 0)
        cnt_row = jnp.zeros((rows, 1), jnp.int32)
        for i in range(segs):
            cnt_row = jnp.where(vrow // SEG == i, near[segs + i], cnt_row)
        keep = jnp.where(lax.rem(vrow, SEG) < cnt_row, 1.0, 0.0)

        def project_point(n, c):
            col = pl.ds(pl.multiple_of(n * 256, 256), 256)
            y = rbuf[:, col].astype(F32) + dot_nn(gbuf[...], wp[:, col])
            obuf[m, :, col] = (y * keep).astype(BF16)
            return c

        lax.fori_loop(0, width // 256, project_point, 0)

        @pl.when(has_next)
        def _():
            block_send(m).start()

            @pl.when(sends_right(m))
            def _():
                halo_send(m, to_slot(m)).start()

        out_copy(m).start()
        return carry

    lax.fori_loop(0, micro, one_block, 0)

    for m in range(micro):
        out_copy(m).wait()

        @pl.when(has_next)
        def _():
            block_send(m).wait_send()

        @pl.when(sends_right(m))
        def _():
            mem_copy(m, to_slot(m)).wait_send()
            rim_copy(m, to_slot(m)).wait_send()

            @pl.when(has_next)
            def _():
                halo_send(m, to_slot(m)).wait_send()

            @pl.when(first_phase)
            def _():
                first_halo(m).wait_send()


def per_device(frames, frame_counts, w_query, w_key, w_value, w_out, conv_kernel, w_point):
    micro, rows, width = frames.shape
    shards = lax.axis_size("tm")
    phases = lax.axis_size("phase")
    dma = pltpu.SemaphoreType.DMA
    any_spec = pl.BlockSpec(memory_space=pl.ANY)
    mat = pltpu.VMEM((width, width), BF16)
    return pl.pallas_call(
        functools.partial(relay_kernel, shards, phases, micro, rows, width),
        out_shape=jax.ShapeDtypeStruct((1, micro, rows, width), BF16),
        in_specs=[pl.BlockSpec(memory_space=pltpu.SMEM)] + [any_spec] * 7,
        out_specs=any_spec,
        scratch_shapes=[
            mat, mat, mat, mat, pltpu.VMEM((KW, width), BF16), mat,
            pltpu.VMEM((micro, LC + rows, width), BF16),
            pltpu.VMEM((LC + rows + 16, width), BF16),
            pltpu.VMEM((LC + rows, width), BF16),
            pltpu.VMEM((LC + rows, width), BF16),
            pltpu.VMEM((rows + 16, width), BF16),
            pltpu.VMEM((rows, width), BF16),
            pltpu.VMEM((rows, width), BF16),
            pltpu.VMEM((SEG + rows, width), F32),
            pltpu.VMEM((rows, width), F32),
            pltpu.VMEM((rows, width), BF16),
            pltpu.VMEM((micro, rows, width), BF16),
            pltpu.VMEM((KW, 8, width), F32),
            pltpu.VMEM((micro, 2 * NMEM, width), F32),
            pltpu.VMEM((micro, 2 * NMEM, width), F32),
            pltpu.VMEM((SEG, width), BF16),
            pltpu.VMEM((SEG, width), BF16),
            pltpu.VMEM((micro, SEG, width), BF16),
            pltpu.VMEM((micro, SEG, width), BF16),
            dma((6,)), dma((micro,)), dma((micro,)),
            dma((micro,)), dma((micro,)), dma((2 * micro,)), dma((micro,)),
            dma((micro,)), dma((micro,)), dma((micro,)), dma((micro,)),
        ],
        compiler_params=pltpu.CompilerParams(
            collective_id=0, has_side_effects=True, vmem_limit_bytes=48 * 1024 * 1024
        ),
    )(frame_counts, frames, w_query, w_key, w_value, w_out, conv_kernel, w_point)


def solution(mesh):
    stage = P("phase", None, None)
    return jax.shard_map(
        per_device,
        mesh=mesh,
        in_specs=(P(None, "tm", None), P(), stage, stage, stage, stage, stage, stage),
        out_specs=P("phase", None, "tm", None),
        check_vma=False,
    )
```

time: 707 us -> 202 us (0.29)
  the two profiles are of different devices: /device:TPU:1 before, /device:TPU:31 now
where the time goes in v1:
time: 202 us
  Pallas kernels  195 us (97%)
  local copies, waits for them, and re-layouts  6.54 us (3%)
    pallas_call x1, Pallas kernels, per_device(): pl.pallas_call(functools.partial(relay_kernel, shards, phases, micro, row...  195 us
    unnamed x11, local copies, waits for them, and re-layouts  6.54 us

profile of v1, /device:TPU:31, one launch (start us, length us, event | category | flops | bytes accessed | tf_op | source)
XLA Modules:
  0.0 201.9 jit_solution(17640600726623972285)
XLA Ops:
  0.0 0.0 copy-start
  0.0 1.6 copy-done
  1.6 0.0 copy-start.1
  1.6 1.6 copy-done.1
  3.2 0.0 copy-start.2
  3.2 1.0 copy-done.2
  4.2 0.0 copy-start.3
  4.2 0.8 copy-done.3
  5.1 0.0 copy-start.4
  5.1 0.7 copy-done.4
  5.7 195.3 %shard_map.82 = bf16[1,2,128,1024]{3,2,1,0:T(8,128)(2,1)S(1)} custom-call(s32[2,128]{1,0:T(2,128)S(1)} %copy-done.4, bf16[2,128,1024]{2,1,0:T(8,128)(2,1)S(1)} %copy-done.2, bf16[1,1024,1024]{2,1,0:T(8,128)(2,1)S(1)} %copy-done, bf16[1,1024,1024]{2,1,0:T(8,128)(2,1)S(1)} %copy-done.1, bf16[1,1024,1024]{2,1,0:T(8,128)(2,1)} %w_value.1, ...), custom_call_target="tpu_custom_call" | custom-call | tf_op jit(solution)/shard_map/pallas_call | solution.py:449
  201.1 0.8 copy.10
Async XLA Ops:
  0.0 1.6 copy-start
  1.6 1.6 copy-start.1
  3.2 1.0 copy-start.2
  4.2 0.8 copy-start.3
  5.1 0.7 copy-start.4

commit v2 on v1

v2 whole, which is shorter than its diff:
```python
import functools

import jax
import jax.numpy as jnp
from jax import lax
from jax.experimental import pallas as pl
from jax.experimental.pallas import tpu as pltpu
from jax.sharding import PartitionSpec as P

HEADS = 16
SEG = 32
LC = 64
NMEM = 4
KW = 31
EPS = 1e-05
NEG = -1e30
PIECES = ((32, 128), (0, 32))
F32 = jnp.float32
BF16 = jnp.bfloat16
MESH = pl.DeviceIdType.MESH


def layer_norm(v):
    width = v.shape[-1]
    c = v - jnp.sum(v, axis=-1, keepdims=True) * (1.0 / width)
    s = jnp.sum(c * c, axis=-1, keepdims=True) * (1.0 / width)
    return c * lax.rsqrt(s + EPS)


def dot_nt(a, b):
    return lax.dot_general(a, b, (((1,), (1,)), ((), ())), preferred_element_type=F32)


def dot_nn(a, b):
    return jnp.dot(a, b, preferred_element_type=F32)


def relay_kernel(
    shards, phases, micro, rows, width,
    counts, frames, w_query, w_key, w_value, w_out, w_conv, w_point,
    out,
    wq, wk, wv, wo, wc, wp,
    xin, nbuf, kbuf, vbuf, qbuf, cbuf, rbuf, cext, dbuf, gbuf, obuf, taps,
    mem_out, mem_in, memk, memv, rim_out, rim_in,
    w_sem, fr_sem, out_sem,
    x_send, x_recv, xh_send, xh_recv, mem_send, mem_recv, rim_send, rim_recv,
):
    t = lax.axis_index("tm")
    p = lax.axis_index("phase")
    segs = rows // SEG
    span_segs = shards * segs
    t_next = lax.rem(t + 1, shards)
    t_prev = lax.rem(t + shards - 1, shards)
    p_next = lax.rem(p + 1, phases)
    p_prev = lax.rem(p + phases - 1, phases)
    first_phase = p == 0
    has_next = p < phases - 1
    last_shard = t == shards - 1
    wrap = jnp.where(last_shard, 1, 0)

    loads = [
        pltpu.make_async_copy(src.at[0], dst, w_sem.at[i])
        for i, (src, dst) in enumerate(
            [(w_key, wk), (w_value, wv), (w_query, wq), (w_out, wo), (w_conv, wc), (w_point, wp)]
        )
    ]

    def frame_load(m):
        return pltpu.make_async_copy(frames.at[m], xin.at[m, pl.ds(LC, rows)], fr_sem.at[m])

    @pl.when(first_phase)
    def _():
        for m in range(micro):
            frame_load(m).start()

    for load in loads:
        load.start()

    barrier = pltpu.get_barrier_semaphore()
    for dt, dp in (
        (t_next, p), (t_prev, p), (t, p_next), (t, p_prev), (t_next, p_next), (t_prev, p_prev)
    ):
        pl.semaphore_signal(barrier, inc=1, device_id=(dt, dp), device_id_type=MESH)
    pl.semaphore_wait(barrier, 6)

    def sends_right(m):
        return jnp.logical_or(t < shards - 1, m < micro - 1)

    def has_left(m):
        return jnp.logical_or(t > 0, m > 0)

    def first_halo(m):
        slot = jnp.minimum(m + wrap, micro - 1)
        return pltpu.make_async_remote_copy(
            src_ref=frames.at[m, pl.ds(rows - LC, LC)],
            dst_ref=xin.at[slot, pl.ds(0, LC)],
            send_sem=xh_send.at[micro + m], recv_sem=xh_recv.at[slot],
            device_id=(t_next, p), device_id_type=MESH,
        )

    def piece_send(m, n):
        lo, hi = PIECES[n]
        return pltpu.make_async_remote_copy(
            src_ref=obuf.at[m, pl.ds(lo, hi - lo)],
            dst_ref=xin.at[m, pl.ds(LC + lo, hi - lo)],
            send_sem=x_send.at[m, n], recv_sem=x_recv.at[m, n],
            device_id=(t, p_next), device_id_type=MESH,
        )

    def to_slot(m):
        return jnp.minimum(m + wrap, micro - 1)

    def halo_send(m, slot):
        return pltpu.make_async_remote_copy(
            src_ref=obuf.at[m, pl.ds(rows - LC, LC)],
            dst_ref=xin.at[slot, pl.ds(0, LC)],
            send_sem=xh_send.at[m], recv_sem=xh_recv.at[slot],
            device_id=(t_next, p_next), device_id_type=MESH,
        )

    def mem_copy(m, slot):
        return pltpu.make_async_remote_copy(
            src_ref=mem_out.at[m], dst_ref=mem_in.at[slot],
            send_sem=mem_send.at[m], recv_sem=mem_recv.at[slot],
            device_id=(t_next, p), device_id_type=MESH,
        )

    def rim_copy(m, slot):
        return pltpu.make_async_remote_copy(
            src_ref=rim_out.at[m], dst_ref=rim_in.at[slot],
            send_sem=rim_send.at[m], recv_sem=rim_recv.at[slot],
            device_id=(t_next, p), device_id_type=MESH,
        )

    def out_copy(m):
        return pltpu.make_async_copy(obuf.at[m], out.at[0, m], out_sem.at[m])

    @pl.when(first_phase)
    def _():
        for m in range(micro):
            @pl.when(sends_right(m))
            def _():
                first_halo(m).start()

    @pl.when(t == 0)
    def _():
        xin[0, 0:LC, :] = jnp.zeros((LC, width), BF16)
        mem_in[0] = jnp.zeros(mem_in.shape[1:], BF16)
        rim_in[0] = jnp.zeros(rim_in.shape[1:], BF16)

    memk[...] = jnp.zeros(memk.shape, F32)
    memv[...] = jnp.zeros(memv.shape, F32)
    loads[4].wait()
    for j in range(KW):
        taps[j] = jnp.broadcast_to(wc[j : j + 1, :].astype(F32), (8, width))

    def count_of(m, rel):
        s = m * span_segs + t * segs + rel
        safe = jnp.maximum(s, 0)
        value = counts[safe // span_segs, lax.rem(safe, span_segs)]
        return jnp.where(s >= 0, value, 0)

    def one_block(m, carry):
        near = [count_of(m, rel) for rel in range(-segs, segs)]
        left = LC // SEG

        total = LC + rows

        def norm_rows(lo, hi):
            for r in range(lo, hi, 16):
                nbuf[r : r + 16, :] = layer_norm(xin[m, r : r + 16, :].astype(F32)).astype(BF16)

        @pl.when(first_phase)
        def _():
            frame_load(m).wait()

        def wait_piece(n):
            @pl.when(jnp.logical_not(first_phase))
            def _():
                piece_send(m, n).wait_recv()

        wait_piece(0)

        def sec_norm2():
            norm_rows(LC + PIECES[0][0], LC + PIECES[0][1])

        sec_norm2()

        @pl.when(has_left(m))
        def _():
            halo_send(m, m).wait_recv()

        def sec_normh():
            norm_rows(0, LC)

        sec_normh()
        wait_piece(1)

        def sec_norm1():
            norm_rows(LC + PIECES[1][0], LC + PIECES[1][1])

        sec_norm1()

        def sec_summary():
            srow = lax.broadcasted_iota(jnp.int32, (16, rows), 0)
            scol = lax.broadcasted_iota(jnp.int32, (16, rows), 1)
            cnt_lane = jnp.zeros((16, rows), jnp.int32)
            cnt_col = jnp.ones((16, 1), jnp.int32)
            crow = lax.broadcasted_iota(jnp.int32, (16, 1), 0)
            for i in range(segs):
                cnt_lane = jnp.where(scol // SEG == i, near[segs + i], cnt_lane)
                cnt_col = jnp.where(crow == i, near[segs + i], cnt_col)
            pick = jnp.logical_and(srow == scol // SEG, lax.rem(scol, SEG) < cnt_lane)
            pick = jnp.where(pick, 1.0, 0.0).astype(BF16)
            summary = dot_nn(pick, nbuf[LC:total, :]) / cnt_col.astype(F32)
            nbuf[total : total + 16, :] = summary.astype(BF16)

        sec_summary()

        @pl.when(m == 0)
        def _():
            for i in (0, 1, 2):
                loads[i].wait()

        def sec_project():
            def project(n, c):
                col = pl.ds(pl.multiple_of(n * 256, 256), 256)
                kbuf[:, col] = dot_nn(nbuf[0:total, :], wk[:, col]).astype(BF16)
                vbuf[:, col] = dot_nn(nbuf[0:total, :], wv[:, col]).astype(BF16)
                qbuf[:, col] = (dot_nn(nbuf[LC : total + 16, :], wq[:, col]).astype(BF16).astype(F32) * 0.125).astype(BF16)
                return c

            lax.fori_loop(0, width // 256, project, 0, unroll=True)

        sec_project()

        def sec_memory():
            nq = segs * HEADS
            hrow = lax.broadcasted_iota(jnp.int32, (HEADS, width), 0)
            hcol = lax.broadcasted_iota(jnp.int32, (HEADS, width), 1) // (width // HEADS)
            head_on = hrow == hcol
            sq = qbuf[rows : rows + 16, :].astype(F32)
            queries = jnp.concatenate(
                [
                    jnp.where(head_on, jnp.broadcast_to(sq[i : i + 1, :], (HEADS, width)), 0.0)
                    for i in range(segs)
                ],
                axis=0,
            ).astype(BF16)
            mrow = lax.broadcasted_iota(jnp.int32, (nq, total), 0) // HEADS
            mcol = lax.broadcasted_iota(jnp.int32, (nq, total), 1)
            mseg = mcol // SEG
            cnt_key = jnp.zeros((nq, total), jnp.int32)
            for i in range(left + segs):
                cnt_key = jnp.where(mseg == i, near[segs - left + i], cnt_key)
            ok = (mseg >= mrow) & (mseg <= mrow + left) & (lax.rem(mcol, SEG) < cnt_key)
            scores = jnp.where(ok, dot_nt(queries, kbuf[...]), NEG)
            expo = jnp.exp(scores - jnp.max(scores, axis=-1, keepdims=True))
            weights = (expo / jnp.sum(expo, axis=-1, keepdims=True)).astype(BF16)
            mixed = dot_nn(weights, vbuf[...])
            memory = jnp.concatenate(
                [
                    jnp.sum(jnp.where(head_on, mixed[i * HEADS : (i + 1) * HEADS, :], 0.0), axis=0, keepdims=True)
                    for i in range(segs)
                ]
                * 4,
                axis=0,
            ).astype(BF16)
            gbuf[0:16, :] = memory

        sec_memory()

        def sec_memproj():
            low = lax.broadcasted_iota(jnp.int32, (2 * NMEM, 256), 0) < NMEM

            def mem_project(n, c):
                col = pl.ds(pl.multiple_of(n * 256, 256), 256)
                mk = dot_nn(gbuf[0:16, :], wk[:, col])[0 : 2 * NMEM]
                mv = dot_nn(gbuf[0:16, :], wv[:, col])[0 : 2 * NMEM]
                mem_out[m, :, col] = jnp.where(low, mk, mv).astype(BF16)
                memk[0 : 2 * NMEM, col] = mk
                memv[0 : 2 * NMEM, col] = mv
                return c

            lax.fori_loop(0, width // 256, mem_project, 0, unroll=True)

        sec_memproj()

        @pl.when(sends_right(m))
        def _():
            mem_copy(m, to_slot(m)).start()

        @pl.when(has_left(m))
        def _():
            mem_copy(m, m).wait_recv()

        def sec_membuf():
            low = lax.broadcasted_iota(jnp.int32, (2 * NMEM, width), 0) < NMEM
            prev = mem_in[m].astype(F32)
            memk[0 : 2 * NMEM, :] = jnp.where(low, prev, memk[0 : 2 * NMEM, :])
            memv[0 : 2 * NMEM, :] = jnp.where(low, pltpu.roll(prev, NMEM, axis=0), memv[0 : 2 * NMEM, :])

        sec_membuf()

        def sec_attend():
            quad = 4
            qw = quad * (width // HEADS)
            win = LC + SEG
            lane = lax.broadcasted_iota(jnp.int32, (1, 128), 1)
            lane_seg = lane // SEG
            biases = []
            for i in range(segs):
                cnt = jnp.zeros((1, 128), jnp.int32)
                for j in range(left + 1):
                    cnt = jnp.where(lane_seg == j, near[segs - left + i + j], cnt)
                okay = (lane < win) & (lax.rem(lane, SEG) < cnt)
                for j in range(NMEM):
                    okay = okay | ((lane == win + i + j) & (near[i + j] > 0))
                biases.append(jnp.where(okay, 0.0, NEG))
            qlane = lax.broadcasted_iota(jnp.int32, (1, qw), 1) // (width // HEADS)
            sel = [jnp.where(qlane == h, 1.0, 0.0).astype(BF16) for h in range(quad)]

            def attend(g, c):
                col = pl.ds(pl.multiple_of(g * qw, qw), qw)
                mk = memk[:, col].astype(BF16)
                mv = memv[:, col].astype(BF16)
                for i in range(segs):
                    q = qbuf[i * SEG : (i + 1) * SEG, col]
                    q4 = jnp.concatenate([q * sel[h] for h in range(quad)], axis=0)
                    ks = jnp.concatenate([kbuf[i * SEG : i * SEG + win, col], mk], axis=0)
                    vs = jnp.concatenate([vbuf[i * SEG : i * SEG + win, col], mv], axis=0)
                    s = dot_nt(q4, ks) + biases[i]
                    e = jnp.exp(s - jnp.max(s, axis=-1, keepdims=True))
                    o = dot_nn(e.astype(BF16), vs) / jnp.sum(e, axis=-1, keepdims=True)
                    ctx = jnp.where(qlane == 0, o[0:SEG], 0.0)
                    for h in range(1, quad):
                        ctx = jnp.where(qlane == h, o[h * SEG : (h + 1) * SEG], ctx)
                    cbuf[i * SEG : (i + 1) * SEG, col] = ctx.astype(BF16)
                return c

            lax.fori_loop(0, width // qw, attend, 0, unroll=True)

        sec_attend()

        @pl.when(m == 0)
        def _():
            loads[3].wait()

        def sec_out():
            def project_out(n, c):
                col = pl.ds(pl.multiple_of(n * 256, 256), 256)
                r = xin[m, LC:total, col].astype(F32) + dot_nn(cbuf[...], wo[:, col])
                rbuf[:, col] = r.astype(BF16)
                return c

            lax.fori_loop(0, width // 256, project_out, 0, unroll=True)

        sec_out()

        def sec_rim():
            def row_mask(i):
                seg = i // 2
                cnt = count_of(m, seg)
                ids = lax.broadcasted_iota(jnp.int32, (16, 1), 0) + lax.rem(i, 2) * 16
                return jnp.where(ids < cnt, 1.0, 0.0)

            def conv_rows(i, c):
                r = pl.multiple_of(i * 16, 16)
                z = (layer_norm(rbuf[pl.ds(r, 16), :].astype(F32)) * row_mask(i)).astype(BF16)
                cext[pl.ds(r + SEG, 16), :] = z.astype(F32)
                return c

            lax.fori_loop(0, rows // 16, conv_rows, 0, unroll=True)
            rim_out[m] = cext[rows : rows + SEG, :].astype(BF16)

        sec_rim()

        @pl.when(sends_right(m))
        def _():
            rim_copy(m, to_slot(m)).start()

        sub = lax.broadcasted_iota(jnp.int32, (8, 128), 0)

        def conv_range(k0, k1):
            def body(cb, c):
                col = pl.ds(pl.multiple_of(cb * 128, 128), 128)
                a = {}

                def get(k):
                    if k not in a:
                        a[k] = cext[8 * k : 8 * k + 8, col]
                    return a[k]

                def tap(o):
                    return taps[o - 2, :, col]

                acc = {}
                for s in range(8):
                    offs = [o for o in range(s, KW + 2, 8) if 2 <= o <= KW + 1]
                    prev = None
                    for k in range(k0, k1 + (1 if s else 0)):
                        y = None
                        for o in offs:
                            term = tap(o) * get(k + o // 8)
                            y = term if y is None else y + term
                        if s == 0:
                            acc[k] = y
                            continue
                        y = pltpu.roll(y, 8 - s, axis=0)
                        if prev is not None:
                            acc[k - 1] = acc[k - 1] + jnp.where(sub < 8 - s, prev, y)
                        prev = y
                for k in range(k0, k1):
                    dbuf[8 * k : 8 * k + 8, col] = acc[k]
                return c

            lax.fori_loop(0, width // 128, body, 0)

        def gate_rows(lo, hi):
            for r in range(lo, hi, 16):
                z = layer_norm(dbuf[r : r + 16, :])
                gbuf[r : r + 16, :] = (z / (1.0 + jnp.exp(-z))).astype(BF16)

        vrow = lax.broadcasted_iota(jnp.int32, (rows, 1), 0)
        cnt_row = jnp.zeros((rows, 1), jnp.int32)
        for i in range(segs):
            cnt_row = jnp.where(vrow // SEG == i, near[segs + i], cnt_row)
        keep = jnp.where(lax.rem(vrow, SEG) < cnt_row, 1.0, 0.0)

        def point_rows(lo, hi):
            def project_point(n, c):
                col = pl.ds(pl.multiple_of(n * 256, 256), 256)
                y = rbuf[lo:hi, col].astype(F32) + dot_nn(gbuf[lo:hi, :], wp[:, col])
                obuf[m, lo:hi, col] = (y * keep[lo:hi]).astype(BF16)
                return c

            lax.fori_loop(0, width // 256, project_point, 0, unroll=True)

        def finish(n):
            lo, hi = PIECES[n]
            conv_range(lo // 8, hi // 8)
            gate_rows(lo, hi)
            point_rows(lo, hi)

        def send_piece(n):
            @pl.when(has_next)
            def _():
                piece_send(m, n).start()

        @pl.when(m == 0)
        def _():
            loads[5].wait()

        def sec_fin0():
            finish(0)

        sec_fin0()
        send_piece(0)

        @pl.when(has_next)
        def _():
            @pl.when(sends_right(m))
            def _():
                halo_send(m, to_slot(m)).start()


        @pl.when(has_left(m))
        def _():
            rim_copy(m, m).wait_recv()

        def sec_fin1():
            cext[0:SEG, :] = rim_in[m].astype(F32)
            finish(1)

        sec_fin1()
        send_piece(1)
        out_copy(m).start()
        return carry

    lax.fori_loop(0, micro, one_block, 0)

    for m in range(micro):
        out_copy(m).wait()

        @pl.when(has_next)
        def _():
            for n in range(len(PIECES)):
                piece_send(m, n).wait_send()

        @pl.when(sends_right(m))
        def _():
            mem_copy(m, to_slot(m)).wait_send()
            rim_copy(m, to_slot(m)).wait_send()

            @pl.when(has_next)
            def _():
                halo_send(m, to_slot(m)).wait_send()

            @pl.when(first_phase)
            def _():
                first_halo(m).wait_send()


def per_device(frames, frame_counts, w_query, w_key, w_value, w_out, conv_kernel, w_point):
    micro, rows, width = frames.shape
    shards = lax.axis_size("tm")
    phases = lax.axis_size("phase")
    dma = pltpu.SemaphoreType.DMA
    any_spec = pl.BlockSpec(memory_space=pltpu.HBM)
    mat = pltpu.VMEM((width, width), BF16)
    return pl.pallas_call(
        functools.partial(relay_kernel, shards, phases, micro, rows, width),
        out_shape=jax.ShapeDtypeStruct((1, micro, rows, width), BF16),
        in_specs=[pl.BlockSpec(memory_space=pltpu.SMEM)] + [any_spec] * 7,
        out_specs=any_spec,
        scratch_shapes=[
            mat, mat, mat, mat, pltpu.VMEM((KW, width), BF16), mat,
            pltpu.VMEM((micro, LC + rows, width), BF16),
            pltpu.VMEM((LC + rows + 16, width), BF16),
            pltpu.VMEM((LC + rows, width), BF16),
            pltpu.VMEM((LC + rows, width), BF16),
            pltpu.VMEM((rows + 16, width), BF16),
            pltpu.VMEM((rows, width), BF16),
            pltpu.VMEM((rows, width), BF16),
            pltpu.VMEM((SEG + rows, width), F32),
            pltpu.VMEM((rows, width), F32),
            pltpu.VMEM((rows, width), BF16),
            pltpu.VMEM((micro, rows, width), BF16),
            pltpu.VMEM((KW, 8, width), F32),
            pltpu.VMEM((micro, 2 * NMEM, width), BF16),
            pltpu.VMEM((micro, 2 * NMEM, width), BF16),
            pltpu.VMEM((SEG, width), F32),
            pltpu.VMEM((SEG, width), F32),
            pltpu.VMEM((micro, SEG, width), BF16),
            pltpu.VMEM((micro, SEG, width), BF16),
            dma((6,)), dma((micro,)), dma((micro,)),
            dma((micro, len(PIECES))), dma((micro, len(PIECES))), dma((2 * micro,)), dma((micro,)),
            dma((micro,)), dma((micro,)), dma((micro,)), dma((micro,)),
        ],
        compiler_params=pltpu.CompilerParams(
            collective_id=0, has_side_effects=True, vmem_limit_bytes=56 * 1024 * 1024
        ),
    )(frame_counts, frames, w_query, w_key, w_value, w_out, conv_kernel, w_point)


def solution(mesh):
    stage = P("phase", None, None)
    return jax.shard_map(
        per_device,
        mesh=mesh,
        in_specs=(P(None, "tm", None), P(), stage, stage, stage, stage, stage, stage),
        out_specs=P("phase", None, "tm", None),
        check_vma=False,
    )
```

time: 202 us -> 138 us (0.68)
  Pallas kernels: 195 us -> 136 us
  local copies, waits for them, and re-layouts: 6.54 us -> 1.87 us
    pallas_call x1, Pallas kernels: 195 us -> 136 us  [per_device(): pl.pallas_call(functools.partial(relay_kernel, shards, phases, micro, row...]
    unnamed x11 -> x1, local copies, waits for them, and re-layouts: 6.54 us -> 1.87 us
where the time goes in v2:
time: 138 us
  Pallas kernels  136 us (99%)
  local copies, waits for them, and re-layouts  1.87 us (1%)
    pallas_call x1, Pallas kernels, per_device(): pl.pallas_call(functools.partial(relay_kernel, shards, phases, micro, row...  136 us

profile of v2, /device:TPU:31, one launch (start us, length us, event | category | flops | bytes accessed | tf_op | source)
XLA Modules:
  0.0 137.6 jit_solution(11475611504509298500)
XLA Ops:
  0.0 135.7 %shard_map.82 = bf16[1,2,128,1024]{3,2,1,0:T(8,128)(2,1)} custom-call(s32[2,128]{1,0:T(2,128)} %counts.1, bf16[2,128,1024]{2,1,0:T(8,128)(2,1)} %frames.1, bf16[1,1024,1024]{2,1,0:T(8,128)(2,1)} %w_query.1, bf16[1,1024,1024]{2,1,0:T(8,128)(2,1)} %w_key.1, bf16[1,1024,1024]{2,1,0:T(8,128)(2,1)} %w_value.1, bf16[1,1024,1024]{2,1,0:T(8,128)(2,1)} %w_out.1, ...), custom_call_target="tpu_custom_call" | custom-call | tf_op jit(solution)/shard_map/pallas_call | solution.py:511
  135.7 1.9 %copy.10 = bf16[1,2,128,1024]{3,2,1,0:T(8,128)(2,1)} copy(bf16[1,2,128,1024]{3,2,1,0:T(8,128)(2,1)} %shard_map.82) | data formatting | bytes 1048576

commit v3 on v2

--- a/solution.py
+++ b/solution.py
@@ -150,9 +150,6 @@
 
     memk[...] = jnp.zeros(memk.shape, F32)
     memv[...] = jnp.zeros(memv.shape, F32)
-    loads[4].wait()
-    for j in range(KW):
-        taps[j] = jnp.broadcast_to(wc[j : j + 1, :].astype(F32), (8, width))
 
     def count_of(m, rel):
         s = m * span_segs + t * segs + rel
@@ -201,7 +198,30 @@
 
         sec_norm1()
 
-        def sec_summary():
+        @pl.when(m == 0)
+        def _():
+            for i in (0, 1, 2):
+                loads[i].wait()
+
+        def project(w, lhs, dst, finish):
+            for n in range(width // 256):
+                col = slice(n * 256, (n + 1) * 256)
+                dst[:, col] = finish(dot_nn(lhs, w[:, col]))
+
+        def plain(r):
+            return r.astype(BF16)
+
+        def scaled(r):
+            return (r.astype(BF16).astype(F32) * 0.125).astype(BF16)
+
+        nq = segs * HEADS
+        hrow = lax.broadcasted_iota(jnp.int32, (HEADS, width), 0)
+        hcol = lax.broadcasted_iota(jnp.int32, (HEADS, width), 1) // (width // HEADS)
+        head_on = hrow == hcol
+
+        def sec_memory():
+            project(wk, nbuf[0:total, :], kbuf, plain)
+
             srow = lax.broadcasted_iota(jnp.int32, (16, rows), 0)
             scol = lax.broadcasted_iota(jnp.int32, (16, rows), 1)
             cnt_lane = jnp.zeros((16, rows), jnp.int32)
@@ -214,31 +234,8 @@
             pick = jnp.where(pick, 1.0, 0.0).astype(BF16)
             summary = dot_nn(pick, nbuf[LC:total, :]) / cnt_col.astype(F32)
             nbuf[total : total + 16, :] = summary.astype(BF16)
-
-        sec_summary()
-
-        @pl.when(m == 0)
-        def _():
-            for i in (0, 1, 2):
-                loads[i].wait()
-
-        def sec_project():
-            def project(n, c):
-                col = pl.ds(pl.multiple_of(n * 256, 256), 256)
-                kbuf[:, col] = dot_nn(nbuf[0:total, :], wk[:, col]).astype(BF16)
-                vbuf[:, col] = dot_nn(nbuf[0:total, :], wv[:, col]).astype(BF16)
-                qbuf[:, col] = (dot_nn(nbuf[LC : total + 16, :], wq[:, col]).astype(BF16).astype(F32) * 0.125).astype(BF16)
-                return c
-
-            lax.fori_loop(0, width // 256, project, 0, unroll=True)
-
-        sec_project()
-
-        def sec_memory():
-            nq = segs * HEADS
-            hrow = lax.broadcasted_iota(jnp.int32, (HEADS, width), 0)
-            hcol = lax.broadcasted_iota(jnp.int32, (HEADS, width), 1) // (width // HEADS)
-            head_on = hrow == hcol
+            project(wq, nbuf[LC : total + 16, :], qbuf, scaled)
+
             sq = qbuf[rows : rows + 16, :].astype(F32)
             queries = jnp.concatenate(
                 [
@@ -255,6 +252,7 @@
                 cnt_key = jnp.where(mseg == i, near[segs - left + i], cnt_key)
             ok = (mseg >= mrow) & (mseg <= mrow + left) & (lax.rem(mcol, SEG) < cnt_key)
             scores = jnp.where(ok, dot_nt(queries, kbuf[...]), NEG)
+            project(wv, nbuf[0:total, :], vbuf, plain)
             expo = jnp.exp(scores - jnp.max(scores, axis=-1, keepdims=True))
             weights = (expo / jnp.sum(expo, axis=-1, keepdims=True)).astype(BF16)
             mixed = dot_nn(weights, vbuf[...])
@@ -289,6 +287,12 @@
         @pl.when(sends_right(m))
         def _():
             mem_copy(m, to_slot(m)).start()
+
+        @pl.when(m == 0)
+        def _():
+            loads[4].wait()
+            for j in range(KW):
+                taps[j] = jnp.broadcast_to(wc[j : j + 1, :].astype(F32), (8, width))
 
         @pl.when(has_left(m))
         def _():
@@ -381,7 +385,7 @@
 
         sub = lax.broadcasted_iota(jnp.int32, (8, 128), 0)
 
-        def conv_range(k0, k1):
+        def conv_range(k0, k1, a0, a1, more, unroll):
             def body(cb, c):
                 col = pl.ds(pl.multiple_of(cb * 128, 128), 128)
                 a = {}
@@ -391,30 +395,40 @@
                         a[k] = cext[8 * k : 8 * k + 8, col]
                     return a[k]
 
-                def tap(o):
-                    return taps[o - 2, :, col]
-
-                acc = {}
+                acc = {k: dbuf[8 * k : 8 * k + 8, col] if more else None for k in range(k0, k1)}
+
+                def add(k, term):
+                    acc[k] = term if acc[k] is None else acc[k] + term
+
                 for s in range(8):
                     offs = [o for o in range(s, KW + 2, 8) if 2 <= o <= KW + 1]
                     prev = None
                     for k in range(k0, k1 + (1 if s else 0)):
                         y = None
                         for o in offs:
-                            term = tap(o) * get(k + o // 8)
-                            y = term if y is None else y + term
+                            if a0 <= k + o // 8 < a1:
+                                term = taps[o - 2, :, col] * get(k + o // 8)
+                                y = term if y is None else y + term
                         if s == 0:
-                            acc[k] = y
+                            if y is not None:
+                                add(k, y)
                             continue
-                        y = pltpu.roll(y, 8 - s, axis=0)
-                        if prev is not None:
-                            acc[k - 1] = acc[k - 1] + jnp.where(sub < 8 - s, prev, y)
+                        if y is not None:
+                            y = pltpu.roll(y, 8 - s, axis=0)
+                        if k > k0 and not (prev is None and y is None):
+                            head = 0.0 if prev is None else prev
+                            tail = 0.0 if y is None else y
+                            add(k - 1, jnp.where(sub < 8 - s, head, tail))
                         prev = y
                 for k in range(k0, k1):
-                    dbuf[8 * k : 8 * k + 8, col] = acc[k]
+                    if acc[k] is not None:
+                        dbuf[8 * k : 8 * k + 8, col] = acc[k]
                 return c
 
-            lax.fori_loop(0, width // 128, body, 0)
+            lax.fori_loop(0, width // 128, body, 0, unroll=unroll)
+
+        first = SEG // 8
+        every = (SEG + rows) // 8
 
         def gate_rows(lo, hi):
             for r in range(lo, hi, 16):
@@ -438,7 +452,6 @@
 
         def finish(n):
             lo, hi = PIECES[n]
-            conv_range(lo // 8, hi // 8)
             gate_rows(lo, hi)
             point_rows(lo, hi)
 
@@ -452,6 +465,7 @@
             loads[5].wait()
 
         def sec_fin0():
+            conv_range(first, rows // 8, first, every, False, 4)
             finish(0)
 
         sec_fin0()
@@ -464,12 +478,18 @@
                 halo_send(m, to_slot(m)).start()
 
 
+        def sec_pre():
+            conv_range(0, first, first, every, False, 4)
+
+        sec_pre()
+
         @pl.when(has_left(m))
         def _():
             rim_copy(m, m).wait_recv()
 
         def sec_fin1():
             cext[0:SEG, :] = rim_in[m].astype(F32)
+            conv_range(0, first, 0, first, True, 4)
             finish(1)
 
         sec_fin1()

time: 138 us -> 133 us (0.964)
  Pallas kernels: 136 us -> 131 us
    pallas_call x1, Pallas kernels: 136 us -> 131 us  [per_device(): pl.pallas_call(functools.partial(relay_kernel, shards, phases, micro, row...]
where the time goes in v3:
time: 133 us
  Pallas kernels  131 us (98%)
  local copies, waits for them, and re-layouts  1.87 us (1%)
    pallas_call x1, Pallas kernels, per_device(): pl.pallas_call(functools.partial(relay_kernel, shards, phases, micro, row...  131 us

profile of v3, /device:TPU:31, one launch (start us, length us, event | category | flops | bytes accessed | tf_op | source)
XLA Modules:
  0.0 133.0 jit_solution(369361619148335072)
XLA Ops:
  0.0 131.1 %shard_map.82 = bf16[1,2,128,1024]{3,2,1,0:T(8,128)(2,1)} custom-call(s32[2,128]{1,0:T(2,128)} %counts.1, bf16[2,128,1024]{2,1,0:T(8,128)(2,1)} %frames.1, bf16[1,1024,1024]{2,1,0:T(8,128)(2,1)} %w_query.1, bf16[1,1024,1024]{2,1,0:T(8,128)(2,1)} %w_key.1, bf16[1,1024,1024]{2,1,0:T(8,128)(2,1)} %w_value.1, bf16[1,1024,1024]{2,1,0:T(8,128)(2,1)} %w_out.1, ...), custom_call_target="tpu_custom_call" | custom-call | tf_op jit(solution)/shard_map/pallas_call | solution.py:531
  131.1 1.9 %copy.10 = bf16[1,2,128,1024]{3,2,1,0:T(8,128)(2,1)} copy(bf16[1,2,128,1024]{3,2,1,0:T(8,128)(2,1)} %shard_map.82) | data formatting | bytes 1048576

commit v4 on v3

--- a/solution.py
+++ b/solution.py
@@ -14,7 +14,7 @@
 KW = 31
 EPS = 1e-05
 NEG = -1e30
-PIECES = ((32, 128), (0, 32))
+PIECES = ((64, 128), (0, 64))
 F32 = jnp.float32
 BF16 = jnp.bfloat16
 MESH = pl.DeviceIdType.MESH
@@ -187,13 +187,10 @@
         def _():
             halo_send(m, m).wait_recv()
 
-        def sec_normh():
+        wait_piece(1)
+
+        def sec_norm1():
             norm_rows(0, LC)
-
-        sec_normh()
-        wait_piece(1)
-
-        def sec_norm1():
             norm_rows(LC + PIECES[1][0], LC + PIECES[1][1])
 
         sec_norm1()
@@ -290,9 +287,63 @@
 
         @pl.when(m == 0)
         def _():
-            loads[4].wait()
+            for i in (3, 4, 5):
+                loads[i].wait()
             for j in range(KW):
                 taps[j] = jnp.broadcast_to(wc[j : j + 1, :].astype(F32), (8, width))
+
+        quad = 4
+        qw = quad * (width // HEADS)
+        win = LC + SEG
+        lane = lax.broadcasted_iota(jnp.int32, (1, 128), 1)
+        lane_seg = lane // SEG
+        biases = []
+        for i in range(segs):
+            cnt = jnp.zeros((1, 128), jnp.int32)
+            for j in range(left + 1):
+                cnt = jnp.where(lane_seg == j, near[segs - left + i + j], cnt)
+            okay = (lane < win) & (lax.rem(lane, SEG) < cnt)
+            for j in range(NMEM):
+                okay = okay | ((lane == win + i + j) & (near[i + j] > 0))
+            biases.append(jnp.where(okay, 0.0, NEG))
+        qlane = lax.broadcasted_iota(jnp.int32, (1, qw), 1) // (width // HEADS)
+        sel = [jnp.where(qlane == h, 1.0, 0.0).astype(BF16) for h in range(quad)]
+
+        def attend(g):
+            col = slice(g * qw, (g + 1) * qw)
+            mk = memk[:, col].astype(BF16)
+            mv = memv[:, col].astype(BF16)
+            for i in range(segs):
+                q = qbuf[i * SEG : (i + 1) * SEG, col]
+                q4 = jnp.concatenate([q * sel[h] for h in range(quad)], axis=0)
+                ks = jnp.concatenate([kbuf[i * SEG : i * SEG + win, col], mk], axis=0)
+                vs = jnp.concatenate([vbuf[i * SEG : i * SEG + win, col], mv], axis=0)
+                s = dot_nt(q4, ks) + biases[i]
+                e = jnp.exp(s - jnp.max(s, axis=-1, keepdims=True))
+                o = dot_nn(e.astype(BF16), vs) / jnp.sum(e, axis=-1, keepdims=True)
+                ctx = jnp.where(qlane == 0, o[0:SEG], 0.0)
+                for h in range(1, quad):
+                    ctx = jnp.where(qlane == h, o[h * SEG : (h + 1) * SEG], ctx)
+                cbuf[i * SEG : (i + 1) * SEG, col] = ctx.astype(BF16)
+
+        def project_out(lo, hi):
+            for n in range(width // 256):
+                col = slice(n * 256, (n + 1) * 256)
+                r = xin[m, LC + lo : LC + hi, col].astype(F32) + dot_nn(cbuf[lo:hi, :], wo[:, col])
+                rbuf[lo:hi, col] = r.astype(BF16)
+
+        vrow = lax.broadcasted_iota(jnp.int32, (rows, 1), 0)
+        cnt_row = jnp.zeros((rows, 1), jnp.int32)
+        for i in range(segs):
+            cnt_row = jnp.where(vrow // SEG == i, near[segs + i], cnt_row)
+        keep = jnp.where(lax.rem(vrow, SEG) < cnt_row, 1.0, 0.0)
+
+        def conv_input(lo, hi):
+            for r in range(lo, hi, 16):
+                z = (layer_norm(rbuf[r : r + 16, :].astype(F32)) * keep[r : r + 16]).astype(BF16)
+                cext[r + SEG : r + SEG + 16, :] = z.astype(F32)
+                if r >= rows - SEG:
+                    rim_out[m, r - rows + SEG : r - rows + SEG + 16, :] = z
 
         @pl.when(has_left(m))
         def _():
@@ -307,77 +358,12 @@
         sec_membuf()
 
         def sec_attend():
-            quad = 4
-            qw = quad * (width // HEADS)
-            win = LC + SEG
-            lane = lax.broadcasted_iota(jnp.int32, (1, 128), 1)
-            lane_seg = lane // SEG
-            biases = []
-            for i in range(segs):
-                cnt = jnp.zeros((1, 128), jnp.int32)
-                for j in range(left + 1):
-                    cnt = jnp.where(lane_seg == j, near[segs - left + i + j], cnt)
-                okay = (lane < win) & (lax.rem(lane, SEG) < cnt)
-                for j in range(NMEM):
-                    okay = okay | ((lane == win + i + j) & (near[i + j] > 0))
-                biases.append(jnp.where(okay, 0.0, NEG))
-            qlane = lax.broadcasted_iota(jnp.int32, (1, qw), 1) // (width // HEADS)
-            sel = [jnp.where(qlane == h, 1.0, 0.0).astype(BF16) for h in range(quad)]
-
-            def attend(g, c):
-                col = pl.ds(pl.multiple_of(g * qw, qw), qw)
-                mk = memk[:, col].astype(BF16)
-                mv = memv[:, col].astype(BF16)
-                for i in range(segs):
-                    q = qbuf[i * SEG : (i + 1) * SEG, col]
-                    q4 = jnp.concatenate([q * sel[h] for h in range(quad)], axis=0)
-                    ks = jnp.concatenate([kbuf[i * SEG : i * SEG + win, col], mk], axis=0)
-                    vs = jnp.concatenate([vbuf[i * SEG : i * SEG + win, col], mv], axis=0)
-                    s = dot_nt(q4, ks) + biases[i]
-                    e = jnp.exp(s - jnp.max(s, axis=-1, keepdims=True))
-                    o = dot_nn(e.astype(BF16), vs) / jnp.sum(e, axis=-1, keepdims=True)
-                    ctx = jnp.where(qlane == 0, o[0:SEG], 0.0)
-                    for h in range(1, quad):
-                        ctx = jnp.where(qlane == h, o[h * SEG : (h + 1) * SEG], ctx)
-                    cbuf[i * SEG : (i + 1) * SEG, col] = ctx.astype(BF16)
-                return c
-
-            lax.fori_loop(0, width // qw, attend, 0, unroll=True)
+            for g in range(width // qw):
+                attend(g)
+            project_out(0, rows)
+            conv_input(0, rows)
 
         sec_attend()
-
-        @pl.when(m == 0)
-        def _():
-            loads[3].wait()
-
-        def sec_out():
-            def project_out(n, c):
-                col = pl.ds(pl.multiple_of(n * 256, 256), 256)
-                r = xin[m, LC:total, col].astype(F32) + dot_nn(cbuf[...], wo[:, col])
-                rbuf[:, col] = r.astype(BF16)
-                return c
-
-            lax.fori_loop(0, width // 256, project_out, 0, unroll=True)
-
-        sec_out()
-
-        def sec_rim():
-            def row_mask(i):
-                seg = i // 2
-                cnt = count_of(m, seg)
-                ids = lax.broadcasted_iota(jnp.int32, (16, 1), 0) + lax.rem(i, 2) * 16
-                return jnp.where(ids < cnt, 1.0, 0.0)
-
-            def conv_rows(i, c):
-                r = pl.multiple_of(i * 16, 16)
-                z = (layer_norm(rbuf[pl.ds(r, 16), :].astype(F32)) * row_mask(i)).astype(BF16)
-                cext[pl.ds(r + SEG, 16), :] = z.astype(F32)
-                return c
-
-            lax.fori_loop(0, rows // 16, conv_rows, 0, unroll=True)
-            rim_out[m] = cext[rows : rows + SEG, :].astype(BF16)
-
-        sec_rim()
 
         @pl.when(sends_right(m))
         def _():
@@ -435,12 +421,6 @@
                 z = layer_norm(dbuf[r : r + 16, :])
                 gbuf[r : r + 16, :] = (z / (1.0 + jnp.exp(-z))).astype(BF16)
 
-        vrow = lax.broadcasted_iota(jnp.int32, (rows, 1), 0)
-        cnt_row = jnp.zeros((rows, 1), jnp.int32)
-        for i in range(segs):
-            cnt_row = jnp.where(vrow // SEG == i, near[segs + i], cnt_row)
-        keep = jnp.where(lax.rem(vrow, SEG) < cnt_row, 1.0, 0.0)
-
         def point_rows(lo, hi):
             def project_point(n, c):
                 col = pl.ds(pl.multiple_of(n * 256, 256), 256)
@@ -460,12 +440,8 @@
             def _():
                 piece_send(m, n).start()
 
-        @pl.when(m == 0)
-        def _():
-            loads[5].wait()
-
         def sec_fin0():
-            conv_range(first, rows // 8, first, every, False, 4)
+            conv_range(PIECES[0][0] // 8, rows // 8, first, every, False, 4)
             finish(0)
 
         sec_fin0()
@@ -479,6 +455,7 @@
 
 
         def sec_pre():
+            conv_range(first, PIECES[0][0] // 8, first, every, False, 4)
             conv_range(0, first, first, every, False, 4)
 
         sec_pre()

time: 133 us -> 130 us (0.977)
  Pallas kernels: 131 us -> 127 us
    pallas_call x1, Pallas kernels: 131 us -> 127 us  [per_device(): pl.pallas_call(functools.partial(relay_kernel, shards, phases, micro, row...]
where the time goes in v4:
time: 130 us; the launch traced here: 129 us
  Pallas kernels  127 us (98%)
  local copies, waits for them, and re-layouts  1.87 us (1%)
    pallas_call x1, Pallas kernels, per_device(): pl.pallas_call(functools.partial(relay_kernel, shards, phases, micro, row...  127 us

profile of v4, /device:TPU:31, one launch (start us, length us, event | category | flops | bytes accessed | tf_op | source)
XLA Modules:
  0.0 129.3 jit_solution(2448359599586740302)
XLA Ops:
  0.0 127.4 %shard_map.82 = bf16[1,2,128,1024]{3,2,1,0:T(8,128)(2,1)} custom-call(s32[2,128]{1,0:T(2,128)} %counts.1, bf16[2,128,1024]{2,1,0:T(8,128)(2,1)} %frames.1, bf16[1,1024,1024]{2,1,0:T(8,128)(2,1)} %w_query.1, bf16[1,1024,1024]{2,1,0:T(8,128)(2,1)} %w_key.1, bf16[1,1024,1024]{2,1,0:T(8,128)(2,1)} %w_value.1, bf16[1,1024,1024]{2,1,0:T(8,128)(2,1)} %w_out.1, ...), custom_call_target="tpu_custom_call" | custom-call | tf_op jit(solution)/shard_map/pallas_call | solution.py:508
  127.4 1.9 %copy.10 = bf16[1,2,128,1024]{3,2,1,0:T(8,128)(2,1)} copy(bf16[1,2,128,1024]{3,2,1,0:T(8,128)(2,1)} %shard_map.82) | data formatting | bytes 1048576

commit v5 on v4

--- a/solution.py
+++ b/solution.py
@@ -58,6 +58,12 @@
     last_shard = t == shards - 1
     wrap = jnp.where(last_shard, 1, 0)
 
+    barrier = pltpu.get_barrier_semaphore()
+    for dt, dp in (
+        (t_next, p), (t_prev, p), (t, p_next), (t, p_prev), (t_next, p_next), (t_prev, p_prev)
+    ):
+        pl.semaphore_signal(barrier, inc=1, device_id=(dt, dp), device_id_type=MESH)
+
     loads = [
         pltpu.make_async_copy(src.at[0], dst, w_sem.at[i])
         for i, (src, dst) in enumerate(
@@ -76,11 +82,6 @@
     for load in loads:
         load.start()
 
-    barrier = pltpu.get_barrier_semaphore()
-    for dt, dp in (
-        (t_next, p), (t_prev, p), (t, p_next), (t, p_prev), (t_next, p_next), (t_prev, p_prev)
-    ):
-        pl.semaphore_signal(barrier, inc=1, device_id=(dt, dp), device_id_type=MESH)
     pl.semaphore_wait(barrier, 6)
 
     def sends_right(m):
@@ -445,18 +446,16 @@
             finish(0)
 
         sec_fin0()
+
+        @pl.when(has_next & sends_right(m))
+        def _():
+            halo_send(m, to_slot(m)).start()
+
         send_piece(0)
 
-        @pl.when(has_next)
-        def _():
-            @pl.when(sends_right(m))
-            def _():
-                halo_send(m, to_slot(m)).start()
-
 
         def sec_pre():
-            conv_range(first, PIECES[0][0] // 8, first, every, False, 4)
-            conv_range(0, first, first, every, False, 4)
+            conv_range(0, PIECES[0][0] // 8, first, every, False, 2)
 
         sec_pre()
 
@@ -535,7 +534,7 @@
             dma((micro,)), dma((micro,)), dma((micro,)), dma((micro,)),
         ],
         compiler_params=pltpu.CompilerParams(
-            collective_id=0, has_side_effects=True, vmem_limit_bytes=56 * 1024 * 1024
+            collective_id=0, has_side_effects=True, vmem_limit_bytes=54528 * 1024
         ),
     )(frame_counts, frames, w_query, w_key, w_value, w_out, conv_kernel, w_point)
 

time: 130 us -> 129 us (level)
  no operation moved by 1% of the time
where the time goes in v5:
time: 129 us
  Pallas kernels  127 us (98%)
  local copies, waits for them, and re-layouts  2.31 us (2%)
    pallas_call x1, Pallas kernels, per_device(): pl.pallas_call(functools.partial(relay_kernel, shards, phases, micro, row...  127 us

profile of v5, /device:TPU:31, one launch (start us, length us, event | category | flops | bytes accessed | tf_op | source)
XLA Modules:
  0.0 128.9 jit_solution(17480437236142281572)
XLA Ops:
  0.0 0.0 copy-start
  0.0 0.8 copy-done
  0.8 0.0 copy-start.1
  0.8 0.7 copy-done.1
  1.5 126.6 %shard_map.82 = bf16[1,2,128,1024]{3,2,1,0:T(8,128)(2,1)S(1)} custom-call(s32[2,128]{1,0:T(2,128)S(1)} %copy-done.1, bf16[2,128,1024]{2,1,0:T(8,128)(2,1)} %frames.1, bf16[1,1024,1024]{2,1,0:T(8,128)(2,1)} %w_query.1, bf16[1,1024,1024]{2,1,0:T(8,128)(2,1)} %w_key.1, bf16[1,1024,1024]{2,1,0:T(8,128)(2,1)} %w_value.1, bf16[1,1024,1024]{2,1,0:T(8,128)(2,1)} %w_out.1, ...), custom_call_target="tpu_custom_call" | custom-call | tf_op jit(solution)/shard_map/pallas_call | solution.py:507
  128.1 0.8 copy.10
Async XLA Ops:
  0.0 0.8 copy-start
  0.8 0.7 copy-start.1

commit v6 on v5

--- a/solution.py
+++ b/solution.py
@@ -210,7 +210,7 @@
             return r.astype(BF16)
 
         def scaled(r):
-            return (r.astype(BF16).astype(F32) * 0.125).astype(BF16)
+            return (r * 0.125).astype(BF16)
 
         nq = segs * HEADS
         hrow = lax.broadcasted_iota(jnp.int32, (HEADS, width), 0)

time: 129 us -> 129 us (level)
  no operation moved by 1% of the time
where the time goes in v6:
time: 129 us
  Pallas kernels  127 us (98%)
  local copies, waits for them, and re-layouts  2.31 us (2%)
    pallas_call x1, Pallas kernels, per_device(): pl.pallas_call(functools.partial(relay_kernel, shards, phases, micro, row...  127 us

profile of v6, /device:TPU:31, one launch (start us, length us, event | category | flops | bytes accessed | tf_op | source)
XLA Modules:
  0.0 128.9 jit_solution(11876595734300074827)
XLA Ops:
  0.0 0.0 copy-start
  0.0 0.8 copy-done
  0.8 0.0 copy-start.1
  0.8 0.7 copy-done.1
  1.5 126.6 %shard_map.82 = bf16[1,2,128,1024]{3,2,1,0:T(8,128)(2,1)S(1)} custom-call(s32[2,128]{1,0:T(2,128)S(1)} %copy-done.1, bf16[2,128,1024]{2,1,0:T(8,128)(2,1)} %frames.1, bf16[1,1024,1024]{2,1,0:T(8,128)(2,1)} %w_query.1, bf16[1,1024,1024]{2,1,0:T(8,128)(2,1)} %w_key.1, bf16[1,1024,1024]{2,1,0:T(8,128)(2,1)} %w_value.1, bf16[1,1024,1024]{2,1,0:T(8,128)(2,1)} %w_out.1, ...), custom_call_target="tpu_custom_call" | custom-call | tf_op jit(solution)/shard_map/pallas_call | solution.py:507
  128.1 0.8 copy.10
Async XLA Ops:
  0.0 0.8 copy-start
  0.8 0.7 copy-start.1
